TPU v7x, 32 devices: a whole 2x2x4 slice. The times are simulated.
32 devices in a mesh: group: 4 (over x, core), dp: 8 (over z, y).
Axes of the slice: x: 2, y: 2, z: 4, core: 2. Of those that a mesh axis runs over, the one named last changes fastest.
Arguments:
- images: float32 [64, 576, 768], P(('group', 'dp')), may hold values from -6 to 6
- cotangent: float32 [64, 576, 768], P(('group', 'dp')), may hold values from -6 to 6
- resolution: int32 [64], P(('group', 'dp')), may hold values from 0 to 2, as said below
- assignment: int32 [64], P(('group', 'dp')), may hold values from 0 to 3, as said below
- counts: int32 [4], replicated, may hold values from 1000 to 63999
- ln1_gain: float32 [768], P('dp'), may hold values from 0.25 to 1.75
- ln1_shift: float32 [768], P('dp'), may hold values from -3 to 3
- qkv_weight: float32 [768, 2304], P('dp'), may hold values from -0.21875 to 0.21875
- qkv_bias: float32 [2304], P('dp'), may hold values from -3 to 3
- rope_freqs: float32 [768], P('dp'), may hold values from -3 to 3
- out_weight: float32 [768, 768], P('dp'), may hold values from -1.75 to 1.75
- out_bias: float32 [768], P('dp'), may hold values from -3 to 3
- ln2_gain: float32 [768], P('dp'), may hold values from 0.25 to 1.75
- ln2_shift: float32 [768], P('dp'), may hold values from -3 to 3
- up_weight: float32 [768, 3072], P('dp'), may hold values from -0.21875 to 0.21875
- up_bias: float32 [3072], P('dp'), may hold values from -3 to 3
- down_weight: float32 [3072, 768], P('dp'), may hold values from -0.109375 to 0.109375
- down_bias: float32 [768], P('dp'), may hold values from -3 to 3
Outputs:
- activations: float32 [64, 576, 768], P(('group', 'dp'))
- input_grad: float32 [64, 576, 768], P(('group', 'dp'))
- grad_ln1_gain: float32 [768], P('dp')
- grad_ln1_shift: float32 [768], P('dp')
- grad_qkv_weight: float32 [768, 2304], P('dp')
- grad_qkv_bias: float32 [2304], P('dp')
- grad_rope_freqs: float32 [768], P('dp')
- grad_out_weight: float32 [768, 768], P('dp')
- grad_out_bias: float32 [768], P('dp')
- grad_ln2_gain: float32 [768], P('dp')
- grad_ln2_shift: float32 [768], P('dp')
- grad_up_weight: float32 [768, 3072], P('dp')
- grad_up_bias: float32 [3072], P('dp')
- grad_down_weight: float32 [3072, 768], P('dp')
- grad_down_bias: float32 [768], P('dp')
Inputs may be any that keep to these rules, and one draw needn't show every extreme that they name: resolution index 0, 1, 2 means 14, 20, 24 patches a side; the first image of each index of group has resolution equal to its group number mod 3, and the group's other images often do. `assignment`: all images on one index of group carry the same group number, and the 4 indices carry different ones.
All inputs are finite; a program needn't handle non-finite values.
Results may differ from a plain program's by a relative error of at most 0.015.
The roundings to bfloat16 on the way count: a program that leaves them out, or rounds other values in their place, can miss the bound.
Values may be sent and summed in bfloat16 or wider, within the bound.
A program may use at most 256 MiB of HBM per device.

v0:
```python
import functools
import math

import jax
import jax.numpy as jnp
from jax import lax
from jax.experimental import pallas as pl
from jax.experimental.pallas import tpu as pltpu
from jax.sharding import PartitionSpec as P

HEADS = 12
HD = 64
SIDE_S = 14
SIDE_M = 20
SIDE_L = 24
SLOT = 576
D = 768
FF = 3072
LN_EPS = 1e-06
MASK_FILL = -1e30
BF = jnp.bfloat16
F32 = jnp.float32
NT = (((1,), (1,)), ((), ()))
NN = (((1,), (0,)), ((), ()))
TN = (((0,), (0,)), ((), ()))
R_G1, R_S1, R_QB, R_FR, R_OB, R_G2, R_S2, R_UB, R_DB, R_ALL = 0, 1, 2, 5, 6, 7, 8, 9, 13, 16
THIRD = 256
LOG2E = math.log2(math.e)


def dot(a, b, dims, precision=None):
    return lax.dot_general(a, b, dims, preferred_element_type=F32, precision=precision)


def vm(n):
    return [pl.BlockSpec(memory_space=pltpu.VMEM)] * n


def norm_stats(x):
    mean = jnp.mean(x, axis=-1, keepdims=True)
    cen = x - mean
    var = jnp.mean(cen * cen, axis=-1, keepdims=True)
    inv = lax.rsqrt(var + LN_EPS)
    return cen * inv, inv


def sincos(x):
    n = jnp.floor(x * (2.0 / math.pi) + 0.5)
    r = x - n * 1.5703125
    r = r - n * 4.837512969970703125e-4
    r = r - n * 7.54978995489188216e-8
    q = n.astype(jnp.int32)
    r2 = r * r
    s = r + r * r2 * (-1.6666654611e-1 + r2 * (8.3321608736e-3 + r2 * -1.9515295891e-4))
    c = 1.0 - 0.5 * r2 + r2 * r2 * (
        4.166664568298827e-2 + r2 * (-1.388731625493765e-3 + r2 * 2.443315711809948e-5)
    )
    odd = (q & 1) == 1
    ss = jnp.where(odd, c, s)
    cc = jnp.where(odd, s, c)
    ss = jnp.where((q & 2) == 2, -ss, ss)
    cc = jnp.where(((q + 1) & 2) == 2, -cc, cc)
    return ss, cc


ERFC = (
    0.07314588129520416,
    -0.30809587240219116,
    0.3798876702785492,
    -0.08230462670326233,
    0.245080828666687,
    0.2054724544286728,
    0.24429383873939514,
    0.242519810795784,
)


def gelu_pair(x):
    z = jnp.abs(x)
    t = 1.0 / (1.0 + (0.43 * math.sqrt(0.5)) * z)
    poly = 0.5 * ERFC[0]
    for c in ERFC[1:]:
        poly = poly * t + 0.5 * c
    bell = jnp.exp2((x * x) * (-0.5 * LOG2E))
    half = poly * t * bell
    cdf = jnp.where(x < 0, half, 1.0 - half)
    return x * cdf, cdf + (x * math.sqrt(0.5 / math.pi)) * bell


def swap_halves(x):
    width = x.shape[-1]
    lane = lax.broadcasted_iota(jnp.int32, (1, width), 1)
    ahead = pltpu.roll(x, width - HD // 2, 1)
    behind = pltpu.roll(x, HD // 2, 1)
    return jnp.where(lane % HD < HD // 2, ahead, behind)


def half_sign(width):
    lane = lax.broadcasted_iota(jnp.int32, (1, width), 1)
    return jnp.where(lane % HD < HD // 2, 1.0, -1.0).astype(F32)


def side_of(res_ref, image):
    res = res_ref[image]
    return jnp.where(res == 0, SIDE_S, jnp.where(res == 1, SIDE_M, SIDE_L))


def device_weight(slots, assign_ref, counts_ref):
    groups = counts_ref.shape[0]
    counts = [jnp.full((1, 128), counts_ref[i], jnp.int32).astype(F32) for i in range(groups)]
    mine = jnp.full((1, 128), assign_ref[0], jnp.int32)
    picked = sum(jnp.where(mine == i, counts[i], 0.0) for i in range(groups))
    return (groups * picked / sum(counts) * (1.0 / math.sqrt(slots)))[:, :1]


def patch_columns(side_ref, image):
    side = jnp.full((SLOT, 128), side_of(side_ref, image), jnp.int32).astype(F32)
    slot = lax.broadcasted_iota(jnp.int32, (SLOT, 128), 0).astype(F32)
    row = jnp.floor((slot + 0.5) / side)
    col = slot - row * side
    valid = slot < side * side
    return col, row, valid


def spread(parity):
    src = lax.broadcasted_iota(jnp.int32, (128, 128), 0)
    lane = lax.broadcasted_iota(jnp.int32, (128, 128), 1)
    return (src == parity * HD + (lane // HD) * (HD // 2) + lane % (HD // 2)).astype(BF)


class Place:
    def __init__(self):
        self.p = lax.axis_index("dp")
        self.g = lax.axis_index("group")
        self.z, self.y = self.p // 2, self.p % 2
        self.x, self.core = self.g // 2, self.g % 2

    def over(self):
        return (self.g, self.p ^ 1)

    def sibling(self):
        return (self.g ^ 1, self.p)

    def across(self):
        return (self.g ^ 2, self.p)

    def line(self):
        return [(self.g, self.p ^ (2 * k)) for k in (1, 2, 3)]

    def partners(self):
        return [self.sibling(), self.across(), self.over()] + self.line()


def remote(src, dst, send, recv, device):
    return pltpu.make_async_remote_copy(
        src_ref=src, dst_ref=dst, send_sem=send, recv_sem=recv, device_id=device, device_id_type=pl.DeviceIdType.MESH
    )


def load(src, dst, sem):
    copy = pltpu.make_async_copy(src, dst, sem)
    copy.start()
    return copy


def greet(devices):
    barrier = pltpu.get_barrier_semaphore()
    for device in devices:
        pl.semaphore_signal(barrier, inc=1, device_id=device, device_id_type=pl.DeviceIdType.MESH)
    pl.semaphore_wait(barrier, len(devices))


def timetable(plan):
    return sorted(((step, name, stage) for name, steps in plan.items() for stage, step in enumerate(steps)), key=lambda r: r[0])


class Moves:
    def __init__(self, items, plan):
        self.items, self.rows = items, timetable(plan)

    def at(self, step):
        for when, name, stage in self.rows:
            if when == step:
                self.items[name].stage(stage)

    def within(self, step, first, last):
        for when in sorted({r[0] for r in self.rows if first <= r[0] <= last}):
            pl.when(step == when)(functools.partial(self.at, when))


class Gather:
    STAGES = 5

    def __init__(self, place, own, full, sems, recv, index):
        self.w, self.own, self.full = place, own, full
        self.rows = full.shape[0] // 8
        self.t = self.rows // 3 if self.rows % 48 == 0 else self.rows * 3 // 8
        self.e = self.rows - 2 * self.t
        self.send, self.sib = sems.at[2 * index], sems.at[2 * index + 1]
        self.recv = recv.at[index]

    def part(self, block, piece, ref=None):
        ref = self.full if ref is None else ref
        first = block * self.rows + piece * self.t
        return ref.at[pl.ds(pl.multiple_of(first, 16), self.e if isinstance(piece, int) else self.t)]

    def push(self, ref, device, index, src=None):
        remote(ref if src is None else src, ref, self.send, self.recv.at[index], device).start()

    def got(self, ref, index):
        remote(ref, ref, self.send, self.recv.at[index], self.w.sibling()).wait_recv()

    def hand(self, ref):
        remote(ref, ref, self.send, self.sib, self.w.sibling()).start()

    def stage(self, number):
        w = self.w
        pl.when(w.core == 0)(lambda: self.step(number, w.x, True))
        pl.when(w.core == 1)(lambda: self.step(number, 2, False))

    def step(self, number, piece, split):
        w = self.w
        if number == 0:
            src = self.part(0, piece, self.own)
            for k in (1, 3, 2):
                self.push(self.part(w.p, piece), (w.g, w.p ^ (2 * k)), w.z, src)
            self.push(self.part(w.p, piece), w.over(), 4 + w.z, src)
        elif number in (1, 2):
            for k in (1, 3, 2) if number == 1 else (0, 1, 3, 2):
                z = w.z ^ k
                block = 2 * z + (w.y if number == 1 else 1 - w.y)
                ref = self.part(block, piece)
                self.got(ref, z if number == 1 else 4 + z)
                if number == 1:
                    self.push(ref, w.over(), 4 + z)
                if split:
                    self.push(ref, w.across(), 8 + block)
                self.hand(ref)
        elif number == 3:
            if split:
                for k in (2, 6, 4, 1, 3, 7, 5):
                    block = w.p ^ k
                    ref = self.part(block, 1 - w.x)
                    self.got(ref, 8 + block)
                    self.hand(ref)
        else:
            for count in (14 * self.t, 14 * self.t) if split else (14 * self.e,):
                done = self.full.at[pl.ds(0, count)]
                remote(done, done, self.send, self.sib, w.sibling()).wait_send()
            came = self.full.at[pl.ds(0, 7 * self.e if split else 14 * self.t)]
            remote(came, came, self.send, self.sib, w.sibling()).wait_recv()


class Reduce:
    STAGES = 7

    def __init__(self, place, src, bufs, out, local, send, recv):
        self.w, self.src, self.out = place, src, out
        self.mine, self.cbuf, self.ybuf, self.zbuf, self.xbuf, self.fbuf = bufs
        self.rows = src.shape[0] // 8
        self.t, self.e = self.split(self.rows)
        self.local, self.send, self.recv = local, send, recv

    @staticmethod
    def split(rows):
        t = rows // 4 if rows % 64 == 0 else rows // 3
        return t, rows - 2 * t

    @classmethod
    def buffers(cls, rows, width):
        t, e = cls.split(rows)
        big = max(2 * t, e)
        sizes = (8 * big, 8 * big, 4 * max(t, e), 4 * max(t, e), 8 * t, max(t, e))
        return [pltpu.VMEM((n, width), BF) for n in sizes]

    def copy(self, src, dst, index, device):
        return remote(src, dst, self.send, self.recv.at[index], device)

    def took(self, ref, index):
        self.copy(ref, ref, index, self.w.sibling()).wait_recv()

    def rows_of(self, ref, first, count):
        return ref.at[pl.ds(pl.multiple_of(first, 16), count)]

    def add(self, target, *terms):
        def body(i, _):
            rows = pl.ds(pl.multiple_of(i * 32, 32), 32)
            total = target[rows].astype(F32)
            for term in terms:
                total = total + term[rows].astype(F32)
            target[rows] = total.astype(BF)
            return 0

        lax.fori_loop(0, target.shape[0] // 32, body, 0)

    def each_core(self, first, second):
        pl.when(self.w.core == 0)(first)
        pl.when(self.w.core == 1)(second)

    def exchange(self, theirs, their_rows, ours, our_rows):
        def body(b, _):
            self.copy(
                self.rows_of(self.src, b * self.rows + theirs, their_rows),
                self.rows_of(self.cbuf, b * their_rows, their_rows),
                0,
                self.w.sibling(),
            ).start()
            pltpu.make_async_copy(
                self.rows_of(self.src, b * self.rows + ours, our_rows),
                self.rows_of(self.mine, b * our_rows, our_rows),
                self.local,
            ).start()
            return 0

        lax.fori_loop(0, 8, body, 0)

    def settle(self, count):
        whole = self.mine.at[pl.ds(0, 8 * count)]
        pltpu.make_async_copy(whole, whole, self.local).wait()
        self.took(self.cbuf.at[pl.ds(0, 8 * count)], 0)
        self.add(whole, self.cbuf)

    def zero_at(self, block, piece):
        return self.rows_of(self.mine, block * 2 * self.t + piece * self.t, self.t)

    def one_at(self, block):
        return self.rows_of(self.mine, block * self.e, self.e)

    def send_y(self, count, at):
        w = self.w

        def body(z, _):
            self.copy(at(2 * z + 1 - w.y), self.rows_of(self.ybuf, z * count, count), 2, w.over()).start()
            return 0

        lax.fori_loop(0, 4, body, 0)

    def take_y(self, count, at):
        self.took(self.ybuf.at[pl.ds(0, 4 * count)], 2)

        def body(z, _):
            self.add(at(2 * z + self.w.y), self.rows_of(self.ybuf, z * count, count))
            return 0

        lax.fori_loop(0, 4, body, 0)

    def send_z(self, count, at):
        w = self.w
        for k in (3, 1, 2):
            z = w.z ^ k
            self.copy(at(2 * z + w.y), self.rows_of(self.zbuf, k * count, count), 3, (w.g, 2 * z + w.y)).start()

    def take_z(self, count, at):
        self.took(self.zbuf.at[pl.ds(0, 3 * count)], 3)
        self.add(at(self.w.p), *[self.rows_of(self.zbuf, k * count, count) for k in (1, 2, 3)])

    def give(self, first, count, value):
        ref = self.out.at[pl.ds(pl.multiple_of(first, 8), count)]
        ref[...] = value
        remote(ref, ref, self.send, self.recv.at[5], self.w.sibling()).start()

    def stage(self, number):
        w, t, e = self.w, self.t, self.e
        x_mine = functools.partial(self.zero_at, piece=w.x)
        x_other = functools.partial(self.zero_at, piece=1 - w.x)
        if number == 0:
            self.each_core(lambda: self.exchange(2 * t, e, 0, 2 * t), lambda: self.exchange(0, 2 * t, 2 * t, e))
        elif number == 1:

            def first():
                self.settle(2 * t)

                def body(b, _):
                    self.copy(x_other(b), self.rows_of(self.xbuf, b * t, t), 1, w.across()).start()
                    return 0

                lax.fori_loop(0, 8, body, 0)

            def second():
                self.settle(e)
                self.send_y(e, self.one_at)

            self.each_core(first, second)
        elif number == 2:

            def first():
                self.took(self.xbuf, 1)

                def body(b, _):
                    self.add(x_mine(b), self.rows_of(self.xbuf, b * t, t))
                    return 0

                lax.fori_loop(0, 8, body, 0)
                self.send_y(t, x_mine)

            def second():
                self.take_y(e, self.one_at)
                self.send_z(e, self.one_at)

            self.each_core(first, second)
        elif number == 3:

            def first():
                self.take_y(t, x_mine)
                self.send_z(t, x_mine)

            def second():
                self.take_z(e, self.one_at)
                self.copy(self.one_at(w.p), self.fbuf.at[pl.ds(0, e)], 4, w.across()).start()

            self.each_core(first, second)
        elif number == 4:

            def first():
                self.take_z(t, x_mine)
                self.copy(x_mine(w.p), self.fbuf.at[pl.ds(0, t)], 4, w.across()).start()
                self.give(w.x * t, t, x_mine(w.p)[...].astype(F32))

            def second():
                self.took(self.fbuf.at[pl.ds(0, e)], 4)
                self.give(2 * t, e, self.one_at(w.p)[...].astype(F32) + self.fbuf[pl.ds(0, e)].astype(F32))

            self.each_core(first, second)
        elif number == 5:

            @pl.when(w.core == 0)
            def _():
                self.took(self.fbuf.at[pl.ds(0, t)], 4)
                self.give((1 - w.x) * t, t, self.fbuf[pl.ds(0, t)].astype(F32))

        else:

            def sent(count):
                while count > 0:
                    now = min(count, self.mine.shape[0])
                    part = self.mine.at[pl.ds(0, now)]
                    remote(part, part, self.send, self.recv.at[0], w.sibling()).wait_send()
                    count -= now

            def came(first, count):
                ref = self.out.at[pl.ds(first, count)]
                remote(ref, ref, self.send, self.recv.at[5], w.sibling()).wait_recv()

            def first():
                came(2 * t, e)
                sent(8 * e + 8 * t + 4 * t + 3 * t + t + 4 * t)

            def second():
                came(0, 2 * t)
                sent(16 * t + 4 * e + 3 * e + e + 2 * e)

            self.each_core(first, second)


class SmallSum:
    HOPS = (4, 2, 4)

    def __init__(self, place, value, bufs, send, recv):
        self.w, self.value, self.bufs, self.send, self.recv = place, value, bufs, send, recv

    def copies(self, hop):
        w = self.w
        for k in range(1, self.HOPS[hop]):
            device = ((w.g ^ k, w.p), (w.g, w.p ^ k), (w.g, w.p ^ (2 * k)))[hop]
            ref = self.bufs.at[4 * hop]
            yield remote(ref, self.bufs.at[4 * hop + k], self.send.at[hop, k], self.recv.at[hop, k], device)

    def stage(self, number):
        w = self.w
        if number > 0:
            hop = number - 1
            for copy in self.copies(hop):
                copy.wait()
            mine = (w.g, w.y, w.z)[hop]
            total = self.bufs[4 * hop + mine]
            for k in range(1, self.HOPS[hop]):
                total = total + self.bufs[4 * hop + (mine ^ k)]
        else:
            total = self.value[...]
        if number == 3:
            self.value[...] = total
        else:
            self.bufs[4 * number] = total
            for copy in self.copies(number):
                copy.start()


def mask_column(side_ref, image):
    side = side_of(side_ref, image)
    slot = lax.broadcasted_iota(jnp.int32, (SLOT, 1), 0)
    return jnp.where(slot < side * side, 0.0, MASK_FILL).astype(F32)


def head_pair(images, step):
    i, j = step % images, step // images
    rows = pl.ds(pl.multiple_of(i * SLOT, SLOT), SLOT)
    return i, rows, pl.multiple_of(j * 128, 128), pl.multiple_of((j // 2) * D + (j % 2) * 128, 128)


def attend_step(images, step, side_ref, qkv_ref, ctx_ref, lse_ref):
    i, rows, c, at = head_pair(images, step)
    q = qkv_ref[rows, pl.ds(at, 128)]
    k = qkv_ref[rows, pl.ds(at + THIRD, 128)]
    v = qkv_ref[rows, pl.ds(at + 2 * THIRD, 128)]
    lane = lax.broadcasted_iota(jnp.int32, (1, 128), 1)
    mask = mask_column(side_ref, i)
    outs, logs = [], []
    for h in range(2):
        qm = jnp.where(lane // HD == h, q, jnp.zeros_like(q))
        s = dot(k, qm, NT) * (LOG2E / math.sqrt(HD)) + mask
        top = jnp.max(s, axis=0, keepdims=True)
        e = jnp.exp2(s - top)
        total = jnp.sum(e, axis=0, keepdims=True)
        p = (e * (1.0 / total)).astype(BF)
        outs.append(dot(p, v, TN))
        logs.append(top + jnp.log2(total))
    ctx_ref[rows, pl.ds(c, 128)] = jnp.where(lane < HD, outs[0], outs[1]).astype(BF)
    lse_ref[step] = jnp.concatenate(logs + [jnp.zeros((6, SLOT), F32)], axis=0)


def norm_rows(images, x_ref, small, norm_ref):
    def body(step, _):
        rows = pl.ds(pl.multiple_of(step * 192, 192), 192)
        unit, _ = norm_stats(x_ref[rows])
        norm_ref[rows] = (unit * small[R_G1 : R_G1 + 1] + small[R_S1 : R_S1 + 1]).astype(BF)
        return 0

    lax.fori_loop(0, images * SLOT // 192, body, 0)


def angle_tables(images, side_ref, small, cos_ref, sin_ref):
    for j in range(D // 128):
        flat = [small[R_FR : R_FR + 1, n + j // 2 * 128 : n + j // 2 * 128 + 128] for n in (0, D // 2)]
        fc, fr = [dot(jnp.broadcast_to(v, (8, 128)).astype(BF), spread(j % 2), NN)[0:1] for v in flat]

        def body(i, _):
            rows = pl.ds(pl.multiple_of(i * SLOT, SLOT), SLOT)
            col, row, _ = patch_columns(side_ref, i)
            sn, cs = sincos(col * fc + row * fr)
            cos_ref[rows, pl.ds(j * 128, 128)] = cs
            sin_ref[rows, pl.ds(j * 128, 128)] = sn * -half_sign(128)
            return 0

        lax.fori_loop(0, images, body, 0)


def project_block(images, c, r, small, w_ref, norm_ref, qkv_ref, cos_ref, sin_ref):
    i, part = r % images, r // images
    rows = pl.ds(pl.multiple_of(i * SLOT, SLOT), SLOT)
    cols = pl.ds(pl.multiple_of(part * THIRD, THIRD), THIRD)
    lanes = pl.ds(pl.multiple_of(c * D + part * THIRD, THIRD), THIRD)
    inner = pl.ds(pl.multiple_of(c * THIRD, THIRD), THIRD)
    raw = dot(norm_ref[rows], w_ref[c, :, cols], NN) + small[pl.ds(R_QB + part, 1), inner]

    @pl.when(part < 2)
    def _():
        turned = raw * cos_ref[rows, inner] + swap_halves(raw) * sin_ref[rows, inner]
        qkv_ref[rows, lanes] = turned.astype(BF)

    @pl.when(part == 2)
    def _():
        qkv_ref[rows, lanes] = raw.astype(BF)


def forward_compute(images, side_ref, x_ref, small, w_ref, qkv, norm, cos, sin, ctx_ref, lse_ref, hooks):
    hooks("start")
    norm_rows(images, x_ref, small, norm)
    hooks("tables")
    angle_tables(images, side_ref, small, cos, sin)
    blocks, pairs = 3 * images, 2 * images

    def body(step, _):
        hooks("step", step)
        c, r = step // (blocks + pairs), step % (blocks + pairs)

        @pl.when(r < blocks)
        def _():
            project_block(images, c, r, small, w_ref, norm, qkv, cos, sin)

        @pl.when(r >= blocks)
        def _():
            attend_step(images, c * pairs + r - blocks, side_ref, qkv, ctx_ref, lse_ref)

        return 0

    lax.fori_loop(0, 3 * (blocks + pairs), body, 0)
    hooks("end")


def forward_plain(images, side_ref, x_ref, small_ref, w_ref, *refs):
    qkv, norm, cos, sin, ctx, lse = refs
    forward_compute(images, side_ref, x_ref, small_ref, w_ref, qkv, norm, cos, sin, ctx, lse, lambda *a: None)


def packed_places(p, dp, sizes):
    run = D // dp
    for first, size in zip(SMALL_ROWS, sizes):
        count = size // run
        yield [(first + (p * count + m) // dp, ((p * count + m) % dp) * run) for m in range(count)]


SMALL_ROWS = (R_G1, R_S1, R_QB, R_FR, R_OB, R_G2, R_S2, R_UB, R_DB)


SINGLES = (R_G1, R_S1, R_FR, R_OB, R_G2, R_S2, R_DB)
MORE = ((2, R_QB, 3, 8), (7, R_UB, 4, 11))


def compact(tinies, ref):
    run = tinies[0].shape[1]
    first = {row: i for i, row in enumerate(SMALL_ROWS)}
    for n, row in enumerate(SINGLES):
        ref[n : n + 1, :run] = tinies[first[row]][...].astype(BF).astype(F32)
    for index, _, count, at in MORE:
        for m in range(count):
            ref[at + m : at + m + 1, :run] = tinies[index][:, m * run : (m + 1) * run].astype(BF).astype(F32)


def expand(parts, small, run):
    small[...] = jnp.zeros_like(small)
    lane = lax.broadcasted_iota(jnp.int32, (1, 128), 1)
    total = None
    for owner, ref in parts:
        wide = jnp.concatenate([jnp.where(lane < run, ref[...], 0.0), jnp.zeros((R_ALL, D - 128), F32)], axis=1)
        term = pltpu.roll(wide[0:8], owner * run, 1)
        total = term if total is None else total + term
        for _, row, count, at in MORE:
            for m in range(count):
                place = owner * count + m
                moved = pltpu.roll(jnp.broadcast_to(wide[at + m : at + m + 1], (8, D)), (place % 8) * run, 1)
                small[pl.ds(row + place // 8, 1), :] += moved[0:1]
    for n, row in enumerate(SINGLES):
        small[row : row + 1] = total[n : n + 1]


def forward_gather(images, side_ref, *refs):
    tinies, x_in, shards_in = refs[0:9], refs[9], refs[10:14]
    qkv_out, norm_out, cos_out, sin_out, ctx, lse, small, wq_out, wo, wu, wd, up_later, down_later = refs[14:27]
    x_ref, qkv, norm, cos, sin, wq, slots, bq, bo, bu, bd, sq, so, su, sd = refs[27:42]
    sems, recv, psend, precv, local, ins = refs[42:]
    w = Place()
    pairs = [(bq.at[c], wq.at[c]) for c in range(3)] + [(bo, wo)]
    pairs += [(own.at[c], full.at[c]) for c in range(PARTS - 1) for own, full in ((bu, wu), (bd, wd))]
    gathers = dict(zip(("q0", "q1", "q2", "o", "u0", "d0", "u1", "d1"), pairs))
    gathers = {k: Gather(w, *v, sems, recv, i) for i, (k, v) in enumerate(gathers.items())}
    moves = Moves(gathers, FORWARD_PLAN)
    peers = [w.p ^ k for k in range(1, 8)]
    keep = {}

    def store(name, src, dst):
        keep[name] = load(src, dst, local.at[len(keep)])

    def qkv_third(c):
        lanes = pl.ds(c * D, D)
        return pltpu.make_async_copy(qkv.at[:, lanes], qkv_out.at[:, lanes], local.at[16 + c])

    def late(number):
        src, dst = ((cos, cos_out), (sin, sin_out), (wq, wq_out))[number]
        return pltpu.make_async_copy(src, dst, local.at[19 + number])

    def own_rows(full):
        count = full.shape[0] // 8
        return full.at[pl.ds(pl.multiple_of(w.p * count, 16), count)]

    def pack_copy(k):
        return remote(slots.at[0], slots.at[k], psend.at[k - 1], precv.at[k - 1], (w.g, peers[k - 1]))

    def hooks(where, step=None):
        if where == "start":
            reads = [
                load(src, dst, ins.at[i])
                for i, (src, dst) in enumerate(zip(shards_in[:1] + (x_in,) + shards_in[1:], (sq, x_ref, so, su, sd)))
            ]
            compact(tinies, slots.at[0])
            greet([(w.g, q) for q in peers] + [w.sibling(), w.across()])
            for k in range(1, 8):
                pack_copy(k).start()
            reads[0].wait()
            for c in range(3):
                for part in range(3):
                    cols = part * D + c * THIRD
                    bq[c, :, part * THIRD : (part + 1) * THIRD] = sq[:, cols : cols + THIRD].astype(BF)
                if c == 0:
                    moves.at(-1)
            for copy in reads[1:]:
                copy.wait()
            bo[...] = so[...].astype(BF)
            for c in range(PARTS):
                for b in range(8):
                    cols = (b * PARTS + c) * 128
                    bu[c, :, b * 128 : (b + 1) * 128] = su[:, cols : cols + 128].astype(BF)
                bd[c] = sd[c * 128 : (c + 1) * 128].astype(BF)
            for i, (own, full) in enumerate(pairs):
                store(i, own, own_rows(full))
            store("up", bu.at[PARTS - 1], up_later)
            store("down", bd.at[PARTS - 1], down_later)
            for k in range(1, 8):
                pack_copy(k).wait()
            expand([(w.p, slots.at[0])] + [(peers[k - 1], slots.at[k]) for k in range(1, 8)], small, D // 8)
            moves.at(0)
        elif where == "tables":
            moves.at(1)
            store("norm", norm, norm_out)
        elif where == "step":

            @pl.when(step == 0)
            def _():
                for i in range(3):
                    keep[i].wait()
                for number in (0, 1):
                    late(number).start()

            moves.within(step + 2, 2, 31)
            for c in (1, 2):

                @pl.when(step == 10 * c)
                def _(c=c):
                    qkv_third(c - 1).start()
                    if c == 2:
                        late(2).start()

        else:
            qkv_third(2).start()
            moves.at(32)
            for c in range(3):
                qkv_third(c).wait()
                late(c).wait()
            for name, copy in keep.items():
                if name not in (0, 1, 2):
                    copy.wait()

    forward_compute(images, side_ref, x_ref, small, wq, qkv, norm, cos, sin, ctx, lse, hooks)


FORWARD_PLAN = {
    "q0": (-1, 1, 2, 2, 2),
    "q1": (0, 2, 9, 11, 12),
    "q2": (1, 4, 10, 16, 19),
    "o": (1, 7, 14, 29, 31),
    "u0": (3, 11, 17, 25, 26),
    "d0": (5, 16, 21, 27, 31),
    "u1": (17, 21, 28, 31, 32),
    "d1": (10, 16, 24, 30, 31),
}


def bias_at(split, step):
    c, k = step // BLOCKS, step % BLOCKS
    if split:
        return (R_UB + k, c * 128), (R_UB + k, D // 2 + c * 128)
    return (R_UB + step // 3, (step % 3) * 256), (R_UB + step // 3, (step % 3) * 256 + 128)


def mlp_compute(images, split, side_ref, scale, cot_ref, ctx_ref, small, wo_ref, wu, wd, refs, outs, hooks):
    mid, n2, n2t, bl, hid, gpre, ubias, gubias = refs
    act, gm, gctx, gdown, gup, gout, gs = outs
    rows_all = images * SLOT
    tile = SLOT // 2
    hooks("start")
    gain = small[R_G2 : R_G2 + 1]
    gs[...] = jnp.zeros_like(gs)
    for step in range(PARTS * BLOCKS):
        for n, (r, l) in enumerate(bias_at(split, step)):
            ubias[step : step + 1, n * 128 : (n + 1) * 128] = small[r : r + 1, l : l + 128]

    def tile_rows(step):
        side = side_of(side_ref, step // 2)
        slot = lax.broadcasted_iota(jnp.int32, (tile, 1), 0) + (step % 2) * tile
        return pl.ds(pl.multiple_of(step * tile, tile), tile), slot < side * side

    def enter(step, _):
        rows, valid = tile_rows(step)
        middle = mid[rows] + (dot(ctx_ref[rows], wo_ref[...], NN) + small[R_OB : R_OB + 1])
        mid[rows] = middle
        act[rows] = middle + small[R_DB : R_DB + 1]
        unit, _ = norm_stats(middle)
        n2[rows] = (unit * gain + small[R_S2 : R_S2 + 1]).astype(BF)
        low = jnp.where(valid, cot_ref[rows], 0.0).astype(BF)
        bl[rows] = low
        gs[R_DB : R_DB + 1] += jnp.sum(low.astype(F32), axis=0, keepdims=True)
        return 0

    lax.fori_loop(0, 2 * images, enter, 0)
    gm[...] = jnp.zeros_like(gm)
    n2t[...] = n2[...].T
    hooks("entered")

    def block(step, _):
        hooks("block", step)
        c, k = step // BLOCKS, step % BLOCKS
        cols = pl.ds(pl.multiple_of(k * 256, 256), 256)
        bias = ubias[pl.ds(step, 1), :]
        wuc = wu[c, :, cols]
        wdc = wd[c, cols, :]
        bsum = None
        for i in range(images):
            rows = pl.ds(i * SLOT, SLOT)
            pre = dot(n2[rows], wuc, NN) + bias
            back = dot(bl[rows], wdc, NT)
            value, slope = gelu_pair(pre)
            hid[rows, cols] = value.astype(BF)
            g = (back * slope).astype(BF)
            gpre[rows, cols] = g
            part = jnp.sum(g.astype(F32), axis=0, keepdims=True)
            bsum = part if bsum is None else bsum + part
        gubias[pl.ds(step, 1), :] = bsum
        gdown[c, cols, :] = (dot(hid[:, cols], bl[...], TN) * scale).astype(BF)
        gup[c, :, cols] = (dot(n2t[...], gpre[:, cols], NN) * scale).astype(BF)

        @pl.when(k == BLOCKS - 1)
        def _():
            def tail(n, _):
                rows = pl.ds(pl.multiple_of(n * tile, tile), tile)
                act[rows] += dot(hid[rows], wd[c], NN)
                gm[rows] += dot(gpre[rows], wu[c], NT)
                return 0

            lax.fori_loop(0, 2 * images, tail, 0)

        return 0

    lax.fori_loop(0, PARTS * BLOCKS, block, 0)
    hooks("blocks")

    def leave(step, _):
        rows, valid = tile_rows(step)
        unit, inv = norm_stats(mid[rows])
        act[rows] = jnp.where(valid, act[rows], 0.0)
        gn = gm[rows]
        gs[R_G2 : R_G2 + 1] += jnp.sum(gn * unit, axis=0, keepdims=True)
        gs[R_S2 : R_S2 + 1] += jnp.sum(gn, axis=0, keepdims=True)
        a = gn * gain
        ma = jnp.mean(a, axis=-1, keepdims=True)
        mu = jnp.mean(a * unit, axis=-1, keepdims=True)
        g = jnp.where(valid, cot_ref[rows], 0.0) + inv * (a - ma - unit * mu)
        gm[rows] = g
        low = g.astype(BF)
        bl[rows] = low
        gs[R_OB : R_OB + 1] += jnp.sum(low.astype(F32), axis=0, keepdims=True)
        gctx[rows] = dot(low, wo_ref[...], NT).astype(BF)
        return 0

    lax.fori_loop(0, 2 * images, leave, 0)
    for step in range(PARTS * BLOCKS):
        for n, (r, l) in enumerate(bias_at(split, step)):
            gs[r : r + 1, l : l + 128] = gubias[step : step + 1, n * 128 : (n + 1) * 128]
    gout[...] = (dot(ctx_ref[...], bl[...], TN) * scale).astype(BF)
    gs[...] = gs[...] * scale
    hooks("end")


def mlp_scratch(rows):
    vmem = pltpu.VMEM
    return (
        [vmem((rows, D), F32), vmem((rows, D), BF), vmem((D, rows), BF), vmem((rows, D), BF)]
        + [vmem((rows, FF // PARTS), BF)] * 2
        + [vmem((16, 256), F32)] * 2
    )


def mlp_plain(images, slots, side_ref, assign_ref, counts_ref, x_ref, cot_ref, ctx_ref, small, wo_ref, wu, wd, *rest):
    outs, refs, sem = rest[0:7], rest[7:15], rest[15]
    load(x_ref, refs[0], sem.at[0]).wait()
    mlp_compute(
        images, False, side_ref, device_weight(slots, assign_ref, counts_ref), cot_ref, ctx_ref, small, wo_ref, wu, wd, refs, outs, lambda *a: None
    )


def mlp_moving(images, slots, side_ref, assign_ref, counts_ref, small, *rest):
    x_in, cot_in, ctx_in, wo_in, wu_in, wd_in, up_later, down_later = rest[0:8]
    act_out, gm_out, gctx_out, gd_out, gu_out, go_out, gs, rd, ru = rest[8:17]
    refs = rest[17:25]
    mid, n2, n2t = refs[0], refs[1], refs[2]
    cot, ctx, wo, wu, wd, act, gm, gd, gu = rest[25:34]
    bufs, (local, sems, recv, rlocal, rsend, rrecv) = rest[34:46], rest[46:52]
    w = Place()
    last = PARTS - 1
    items = {
        "u": Gather(w, up_later, wu.at[last], sems, recv, 0),
        "d": Gather(w, down_later, wd.at[last], sems, recv, 1),
        "rd": Reduce(w, gd.at[0], bufs[0:6], rd, rlocal.at[0], rsend.at[0], rrecv.at[0]),
        "ru": Reduce(w, gu.at[0], bufs[6:12], ru, rlocal.at[1], rsend.at[1], rrecv.at[1]),
    }
    moves = Moves(items, MLP_PLAN)
    keep = []

    def move(src, dst):
        keep.append(load(src, dst, local.at[len(keep)]))
        return keep[-1]

    def hooks(where, step=None):
        if where == "start":
            move(ctx_in, ctx), move(x_in, mid), move(wo_in, wo), move(cot_in, cot)
            for c in range(last):
                move(wu_in.at[c], wu.at[c])
                move(wd_in.at[c], wd.at[c])
            for own, full in ((up_later, wu), (down_later, wd)):
                count = full.shape[1] // 8
                move(own, full.at[last, pl.ds(pl.multiple_of(w.p * count, 16), count)])
            greet(w.partners())
            moves.at(0)
            for copy in keep[:4]:
                copy.wait()
        elif where == "entered":
            for copy in keep[4:]:
                copy.wait()
            keep.clear()
        elif where == "block":
            moves.within(step + 1, 1, 12)
        elif where == "blocks":
            for c in (1, 2):
                move(gd.at[c], gd_out.at[c - 1])
                move(gu.at[c], gu_out.at[c - 1])
            moves.at(13)
        else:
            move(act, act_out)
            move(gm, gm_out)
            move(n2, gctx_out)
            move(n2t.at[:, pl.ds(0, D)], go_out)
            moves.at(14)
            for copy in keep:
                copy.wait()

    mlp_compute(
        images,
        True,
        side_ref,
        device_weight(slots, assign_ref, counts_ref),
        cot,
        ctx,
        small,
        wo,
        wu,
        wd,
        refs,
        (act, gm, n2, gd, gu, n2t.at[:, pl.ds(0, D)], gs),
        hooks,
    )


MLP_PLAN = {
    "u": (1, 4, 7, 9, 9),
    "d": (0, 1, 4, 6, 8),
    "rd": (5, 6, 8, 9, 11, 13, 14),
    "ru": (6, 8, 10, 12, 13, 14, 14),
}


PARTS = 3
BLOCKS = 4


def attend_back_step(images, step, side_ref, qkv_ref, gctx_ref, lse_ref, cos_ref, sin_ref, gproj_ref, gs_ref, gf_ref):
    i, rows, c, at = head_pair(images, step)
    q = qkv_ref[rows, pl.ds(at, 128)]
    k = qkv_ref[rows, pl.ds(at + THIRD, 128)]
    v = qkv_ref[rows, pl.ds(at + 2 * THIRD, 128)]
    go = gctx_ref[rows, pl.ds(c, 128)]
    lane = lax.broadcasted_iota(jnp.int32, (1, 128), 1)
    mask = mask_column(side_ref, i)
    lse = lse_ref[step]
    dq, dk, dv = [], [], []
    for h in range(2):
        mine = lane // HD == h
        qm = jnp.where(mine, q, jnp.zeros_like(q))
        gom = jnp.where(mine, go, jnp.zeros_like(go))
        s = dot(k, qm, NT) * (LOG2E / math.sqrt(HD)) + mask
        p = jnp.exp2(s - lse[h : h + 1])
        dp = dot(v, gom, NT)
        dv.append(dot(p.astype(BF), go, NN))
        t = p * dp
        ds = (t - p * jnp.sum(t, axis=0, keepdims=True)).astype(BF)
        dk.append(dot(ds, q, NN))
        dq.append(dot(ds, k, TN))
    first = lane < HD
    cs = cos_ref[rows, pl.ds(c, 128)]
    sn = sin_ref[rows, pl.ds(c, 128)]
    angle = None
    for n, (pair, rot) in enumerate(((dq, q), (dk, k))):
        e = jnp.where(first, pair[0], pair[1]) * (1.0 / math.sqrt(HD))
        other = swap_halves(e)
        back = (e * cs - other * sn).astype(BF)
        gproj_ref[rows, pl.ds(at + n * THIRD, 128)] = back
        gs_ref[pl.ds(R_QB + n, 1), pl.ds(c, 128)] += jnp.sum(back.astype(F32), axis=0, keepdims=True)
        term = rot.astype(F32) * other
        angle = term if angle is None else angle + term
    gv = jnp.where(first, dv[0], dv[1]).astype(BF)
    gproj_ref[rows, pl.ds(at + 2 * THIRD, 128)] = gv
    gs_ref[R_QB + 2 : R_QB + 3, pl.ds(c, 128)] += jnp.sum(gv.astype(F32), axis=0, keepdims=True)
    angle = angle * half_sign(128)
    col, row, _ = patch_columns(side_ref, i)
    gf_ref[0:1, pl.ds(c, 128)] += jnp.sum(angle * col, axis=0, keepdims=True)
    gf_ref[1:2, pl.ds(c, 128)] += jnp.sum(angle * row, axis=0, keepdims=True)


def freq_row(gf_ref, gs_ref):
    for m in range(D // 128):
        which = m // 3
        total = None
        for parity in (0, 1):
            lanes = 2 * (m % 3) + parity
            value = gf_ref[which : which + 1, lanes * 128 : lanes * 128 + 128]
            for _ in range(3):
                term = value.astype(BF)
                value = value - term.astype(F32)
                moved = dot(jnp.broadcast_to(term, (8, 128)), spread(parity), NT)[0:1]
                total = moved if total is None else total + moved
        gs_ref[R_FR : R_FR + 1, m * 128 : m * 128 + 128] = total


def weight_third(c, scale, norm_ref, gproj_ref, gw_ref):
    def block(j, _):
        lanes = pl.ds(pl.multiple_of(j * THIRD, THIRD), THIRD)
        full = pl.ds(pl.multiple_of(c * D + j * THIRD, THIRD), THIRD)
        gw_ref[:, lanes] = (dot(norm_ref[...], gproj_ref[:, full], TN) * scale).astype(BF)
        return 0

    lax.fori_loop(0, 3, block, 0)


def attend_back_compute(images, thirds, side_ref, scale, ins, norm, gproj, gws, gs_ref, gf_ref, hooks):
    hooks("start")
    gs_ref[...] = jnp.zeros_like(gs_ref)
    gf_ref[...] = jnp.zeros_like(gf_ref)

    def body(step, _):
        hooks("step", step)
        attend_back_step(images, step, side_ref, *ins, gproj, gs_ref, gf_ref)
        for c in range(thirds):

            @pl.when(step == 2 * images * (c + 1) - 1)
            def _(c=c):
                weight_third(c, scale, norm, gproj, gws.at[c])

        return 0

    lax.fori_loop(0, images * HEADS // 2, body, 0)
    freq_row(gf_ref, gs_ref)
    hooks("end")


def attend_back_plain(images, slots, side_ref, assign_ref, counts_ref, *refs):
    ins, norm, (gproj, gws, gs, gf) = refs[0:5], refs[5], refs[6:10]
    attend_back_compute(images, 3, side_ref, device_weight(slots, assign_ref, counts_ref), ins, norm, gproj, gws, gs, gf, lambda *a: None)


def attend_back_reduce(images, slots, side_ref, assign_ref, counts_ref, *refs):
    ins_in, norm_in, (gd, gu, go) = refs[0:5], refs[5], refs[6:9]
    gproj_out, gs, outs = refs[9], refs[10], refs[11:18]
    ins, norm, gproj, gws, gf = refs[18:23], refs[23], refs[24], refs[25], refs[26]
    bufs, (load_sems, local, send, recv) = refs[27:69], refs[69:73]
    w = Place()
    srcs = (gd.at[0], gu.at[0], gd.at[1], gu.at[1], go, gws.at[0], gws.at[1])
    items = {
        name: Reduce(w, srcs[i], bufs[6 * i : 6 * i + 6], outs[i], local.at[i], send.at[i], recv.at[i])
        for i, name in enumerate(BACK_PLAN)
    }
    moves = Moves(items, BACK_PLAN)

    def hooks(where, step=None):
        if where == "start":
            copies = [load(src, dst, load_sems.at[i]) for i, (src, dst) in enumerate(zip(ins_in + (norm_in,), ins + (norm,)))]
            greet(w.partners())
            moves.at(0)
            for copy in copies:
                copy.wait()
        elif where == "step":
            moves.within(step + 1, 1, 12)
        else:
            copy = load(gproj, gproj_out, load_sems.at[0])
            moves.at(13)
            moves.at(14)
            copy.wait()

    attend_back_compute(images, 2, side_ref, device_weight(slots, assign_ref, counts_ref), ins, norm, gproj, gws, gs, gf, hooks)


BACK_PLAN = {
    "d1": (3, 4, 7, 9, 11, 14, 14),
    "u1": (0, 2, 4, 8, 10, 13, 13),
    "d2": (1, 3, 5, 8, 10, 12, 12),
    "u2": (3, 7, 9, 10, 13, 14, 14),
    "o": (0, 3, 7, 9, 11, 12, 13),
    "q0": (5, 8, 10, 12, 13, 14, 14),
    "q1": (9, 9, 11, 12, 13, 14, 14),
}


def qkv_back_compute(images, x_ref, gproj_ref, gm_ref, small_ref, w_ref, gs_in, gin_ref, gs_ref, hooks):
    hooks("start")
    gain = small_ref[R_G1 : R_G1 + 1]
    gs_ref[...] = gs_in[...]
    tile = SLOT // 2

    def body(step, _):
        hooks("tile", step)
        rows = pl.ds(pl.multiple_of(step * tile, tile), tile)
        unit, inv = norm_stats(x_ref[rows])
        gn = None
        for c in range(3):
            term = dot(gproj_ref[rows, c * D : (c + 1) * D], w_ref[c], NT)
            gn = term if gn is None else gn + term
        gs_ref[R_G1 : R_G1 + 1] += jnp.sum(gn * unit, axis=0, keepdims=True)
        gs_ref[R_S1 : R_S1 + 1] += jnp.sum(gn, axis=0, keepdims=True)
        a = gn * gain
        ma = jnp.mean(a, axis=-1, keepdims=True)
        mu = jnp.mean(a * unit, axis=-1, keepdims=True)
        gin_ref[rows] = gm_ref[rows] + inv * (a - ma - unit * mu)
        return 0

    lax.fori_loop(0, 2 * images, body, 0)
    hooks("end")


def qkv_back_plain(images, slots, assign_ref, counts_ref, x_ref, gproj_ref, gm_ref, small_ref, w_ref, gs_in, gin, gs):
    def hooks(where, index=None):
        if where == "end":
            gs[...] = gs[...] * device_weight(slots, assign_ref, counts_ref)

    qkv_back_compute(images, x_ref, gproj_ref, gm_ref, small_ref, w_ref, gs_in, gin, gs, hooks)


def qkv_back_reduce(images, slots, assign_ref, counts_ref, small_ref, gs_att, gs_mlp, *refs):
    ins_in, (gin, gs, out) = refs[0:5], refs[5:8]
    norm, gproj, x, w_ref, gm = refs[8:13]
    gw, bufs, tinybufs, (load_sems, local, send, recv, ssend, srecv) = refs[13], refs[14:20], refs[20], refs[21:27]
    w = Place()
    last = Reduce(w, gw, bufs, out, local, send, recv)
    tiny = SmallSum(w, gs, tinybufs, ssend, srecv)
    weight = device_weight(slots, assign_ref, counts_ref)

    def hooks(where, index=None):
        if where == "start":
            copies = [load(src, dst, load_sems.at[i]) for i, (src, dst) in enumerate(zip(ins_in, refs[8:13]))]
            greet(w.partners() + [(w.g ^ 3, w.p)])
            copies[0].wait()
            copies[1].wait()
            weight_third(2, weight, norm, gproj, gw)
            last.stage(0)
            for copy in copies[2:]:
                copy.wait()
        elif where == "tile":
            for number, when in ((1, 1), (2, 3)):

                @pl.when(index == when)
                def _(number=number):
                    last.stage(number)

        else:
            gs[...] = gs[...] * weight + gs_mlp[...]
            tiny.stage(0)
            last.stage(3)
            tiny.stage(1)
            last.stage(4)
            tiny.stage(2)
            last.stage(5)
            tiny.stage(3)
            last.stage(6)

    qkv_back_compute(images, x, gproj, gm, small_ref, w_ref, gs_att, gin, gs, hooks)


def finish_kernel(dp, p_axis, gs, act_in, gin_in, rout_in, *refs):
    rd, ru, rq = refs[0:3], refs[3:6], refs[6:9]
    act, gin, rqkv, rout, rup, rdown, sems = refs[9], refs[10], *refs[11:15], refs[-1]
    tinies = refs[15:-2]
    stage = refs[-2]
    ins = [load(act_in, stage.at[0], sems.at[0]), load(gin_in, stage.at[1], sems.at[1])]
    p = lax.axis_index(p_axis)
    run = D // dp
    for out, places in zip(tinies, packed_places(p, dp, [t.shape[0] for t in tinies])):
        for m, (row, lane) in enumerate(places):
            whole = jnp.broadcast_to(gs[pl.ds(row, 1), :], (8, D))
            out[pl.ds(m * run, run)] = pltpu.roll(whole, D - lane, 1)[0, :run]
    copies = []
    for n, dst in enumerate((act, gin)):
        ins[n].wait()
        copies.append(load(stage.at[n], dst, sems.at[n]))
    rout[...] = rout_in[...]
    for c in range(3):
        rdown[c * rd[c].shape[0] : (c + 1) * rd[c].shape[0]] = rd[c][...]
        for b in range(dp):
            rup[:, (b * 3 + c) * 128 : (b * 3 + c + 1) * 128] = ru[c][:, b * 128 : (b + 1) * 128]
        for part in range(3):
            cols = part * D + c * THIRD
            rqkv[:, cols : cols + THIRD] = rq[c][:, part * THIRD : (part + 1) * THIRD]
    for copy in copies:
        copy.wait()


def params(mb=56):
    return pltpu.CompilerParams(vmem_limit_bytes=mb << 20)


def place_rows(p, dp, vec):
    n = vec.shape[0]
    whole = jnp.tile(vec, dp)
    owner = jnp.arange(n * dp, dtype=jnp.int32) // n
    return jnp.where(owner == p, whole, 0.0).reshape(-1, D)


def on_device(
    fast,
    images,
    cotangent,
    resolution,
    assignment,
    counts,
    ln1_gain,
    ln1_shift,
    qkv_weight,
    qkv_bias,
    rope_freqs,
    out_weight,
    out_bias,
    ln2_gain,
    ln2_shift,
    up_weight,
    up_bias,
    down_weight,
    down_bias,
):
    p = lax.axis_index("dp")
    dp = lax.axis_size("dp")
    n = images.shape[0]
    rows = n * SLOT
    x = images.reshape(rows, D)
    cot = cotangent.reshape(rows, D)
    vectors = (ln1_gain, ln1_shift, qkv_bias, rope_freqs, out_bias, ln2_gain, ln2_shift, up_bias, down_bias)
    slots = dp * rows
    sds = jax.ShapeDtypeStruct
    smem = pl.BlockSpec(memory_space=pltpu.SMEM)
    anyw = pl.BlockSpec(memory_space=pl.ANY)
    kept = [
        sds((rows, 3 * D), BF),
        sds((rows, D), BF),
        sds((rows, D), F32),
        sds((rows, D), F32),
        sds((rows, D), BF),
        sds((n * HEADS // 2, 8, SLOT), F32),
    ]
    weights = (qkv_weight, out_weight, up_weight, down_weight)
    dma = pltpu.SemaphoreType.DMA
    vmem = pltpu.VMEM

    def moving(number, mb):
        return pltpu.CompilerParams(vmem_limit_bytes=mb << 20, collective_id=number, has_side_effects=True)

    part = FF // PARTS
    if fast:
        later = [sds((D // dp, part), BF), sds((part // dp, D), BF)]
        fulls = [sds((3, D, D), BF), sds((D, D), BF), sds((PARTS - 1, D, part), BF), sds((PARTS - 1, part, D), BF)]
        outs = pl.pallas_call(
            functools.partial(forward_gather, n),
            out_shape=kept + [sds((R_ALL, D), F32)] + fulls + later,
            in_specs=[smem] + vm(9) + [anyw] * 5,
            out_specs=[anyw] * 4 + vm(3) + [anyw] * 6,
            scratch_shapes=[
                vmem((rows, D), F32),
                vmem((rows, 3 * D), BF),
                vmem((rows, D), BF),
                vmem((rows, D), F32),
                vmem((rows, D), F32),
                vmem((3, D, D), BF),
                vmem((8, R_ALL, 128), F32),
                vmem((3, D // dp, D), BF),
                vmem((D // dp, D), BF),
                vmem((PARTS, D // dp, part), BF),
                vmem((PARTS, part // dp, D), BF),
            ]
            + [vmem(v.shape, F32) for v in weights]
            + [
                dma((16,)),
                dma((8, 16)),
                dma((7,)),
                dma((7,)),
                dma((22,)),
                dma((5,)),
            ],
            compiler_params=moving(0, 56),
            name="forward",
        )(resolution, *[v.reshape(1, -1) for v in vectors], x, *weights)
        qkv, norm1, cos, sin, ctx, lse, small, wqkv, wo, wu, wd, up_later, down_later = outs
    else:
        packed = [place_rows(p, dp, lax.reduce_precision(v, 8, 7)) for v in vectors]
        small = lax.psum(jnp.concatenate(packed + [jnp.zeros((2, D), F32)], axis=0), "dp")
        wqkv, wo, wu, wd = [lax.all_gather(v.astype(BF), "dp", axis=0, tiled=True) for v in weights]
        wqkv = wqkv.reshape(D, 3, 3, THIRD).transpose(2, 0, 1, 3).reshape(3, D, D)
        wu = wu.reshape(D, PARTS, part).transpose(1, 0, 2)
        wd = wd.reshape(PARTS, part, D)
        qkv, norm1, cos, sin, ctx, lse = pl.pallas_call(
            functools.partial(forward_plain, n),
            out_shape=kept,
            in_specs=[smem] + vm(3),
            out_specs=vm(6),
            compiler_params=params(),
            name="forward",
        )(resolution, x, small, wqkv)

    grads = [sds((PARTS, part, D), BF), sds((PARTS, D, part), BF), sds((D, D), BF)]
    rest = [sds((R_ALL, D), F32)]
    firsts = [sds((rows, D), F32), sds((rows, D), F32), sds((rows, D), BF)]
    tables = [vmem((rows, 3 * D), BF), vmem((rows, D), BF), vmem((n * HEADS // 2, 8, SLOT), F32)]
    tables += [vmem((rows, D), F32)] * 2
    gproj_shape = sds((rows, 3 * D), BF)
    if fast:
        sizes = [(part // dp, D), (D // dp, part)]
        act, gm, gctx, gdown, gup, gout, gs_mlp, rdown0, rup0 = pl.pallas_call(
            functools.partial(mlp_moving, n, slots),
            out_shape=firsts
            + [sds((PARTS - 1,) + g.shape[1:], BF) for g in grads[:2]]
            + grads[2:]
            + rest
            + [sds(z, F32) for z in sizes],
            in_specs=[smem] * 3 + vm(1) + [anyw] * 8,
            out_specs=[anyw] * 6 + vm(3),
            scratch_shapes=mlp_scratch(rows)
            + [
                vmem((rows, D), F32),
                vmem((rows, D), BF),
                vmem((D, D), BF),
                vmem((PARTS, D, part), BF),
                vmem((PARTS, part, D), BF),
                vmem((rows, D), F32),
                vmem((rows, D), F32),
                vmem((PARTS, part, D), BF),
                vmem((PARTS, D, part), BF),
            ]
            + sum([Reduce.buffers(*z) for z in sizes], [])
            + [dma((12,)), dma((4,)), dma((2, 16)), dma((2,)), dma((2,)), dma((2, 6))],
            compiler_params=moving(3, 63),
            name="mlp",
        )(resolution, assignment, counts, small, x, cot, ctx, wo, wu, wd, up_later, down_later)
        third = (D // dp, D)
        sizes = sizes + sizes + [third] * 3
        gproj, gs_att, rdown1, rup1, rdown2, rup2, rout, rq0, rq1 = pl.pallas_call(
            functools.partial(attend_back_reduce, n, slots),
            out_shape=[gproj_shape] + rest + [sds(z, F32) for z in sizes],
            in_specs=[smem] * 3 + [anyw] * 9,
            out_specs=[anyw] + vm(8),
            scratch_shapes=tables
            + [vmem((rows, D), BF), vmem((rows, 3 * D), BF), vmem((2, D, D), BF), vmem((8, D), F32)]
            + sum([Reduce.buffers(*z) for z in sizes], [])
            + [dma((6,)), dma((7,)), dma((7,)), dma((7, 6))],
            compiler_params=moving(1, 62),
            name="attend_back",
        )(resolution, assignment, counts, qkv, gctx, lse, cos, sin, norm1, gdown, gup, gout)
        gin, gs, rq2 = pl.pallas_call(
            functools.partial(qkv_back_reduce, n, slots),
            out_shape=[sds((rows, D), F32)] + rest + [sds(third, F32)],
            in_specs=[smem] * 2 + vm(3) + [anyw] * 5,
            out_specs=vm(3),
            scratch_shapes=[
                vmem((rows, D), BF),
                vmem((rows, 3 * D), BF),
                vmem((rows, D), F32),
                vmem((3, D, D), BF),
                vmem((rows, D), F32),
                vmem((D, D), BF),
            ]
            + Reduce.buffers(*third)
            + [vmem((12, R_ALL, D), F32), dma((5,)), dma, dma, dma((6,)), dma((3, 4)), dma((3, 4))],
            compiler_params=moving(2, 60),
            name="project_back",
        )(assignment, counts, small, gs_att, gs_mlp, norm1, gproj, x, wqkv, gm)

        matrices = (qkv_weight, out_weight, up_weight, down_weight)
        act, gin, rqkv, rout, rup, rdown, *tinies = pl.pallas_call(
            functools.partial(finish_kernel, dp, "dp"),
            out_shape=[sds((rows, D), F32)] * 2 + [sds(v.shape, F32) for v in matrices + vectors],
            in_specs=vm(1) + [anyw] * 2 + vm(10),
            out_specs=[anyw] * 2 + vm(13),
            scratch_shapes=[vmem((2, rows, D), F32), dma((2,))],
            compiler_params=params(),
            name="finish",
        )(gs, act, gin, rout, rdown0, rdown1, rdown2, rup0, rup1, rup2, rq0, rq1, rq2)
    else:
        act, gm, gctx, gdown, gup, gout, gs_mlp = pl.pallas_call(
            functools.partial(mlp_plain, n, slots),
            out_shape=firsts + grads + rest,
            in_specs=[smem] * 3 + [anyw] + vm(6),
            out_specs=vm(7),
            scratch_shapes=mlp_scratch(rows) + [dma((1,))],
            compiler_params=params(63),
            name="mlp",
        )(resolution, assignment, counts, x, cot, ctx, small, wo, wu, wd)
        gproj, gqkv, gs_att = pl.pallas_call(
            functools.partial(attend_back_plain, n, slots),
            out_shape=[gproj_shape, sds((3, D, D), BF)] + rest,
            in_specs=[smem] * 3 + vm(6),
            out_specs=vm(3),
            scratch_shapes=[vmem((8, D), F32)],
            compiler_params=params(),
            name="attend_back",
        )(resolution, assignment, counts, qkv, gctx, lse, cos, sin, norm1)
        gin, gs_qkv = pl.pallas_call(
            functools.partial(qkv_back_plain, n, slots),
            out_shape=[sds((rows, D), F32)] + rest,
            in_specs=[smem] * 2 + vm(6),
            out_specs=vm(2),
            compiler_params=params(),
            name="project_back",
        )(assignment, counts, x, gproj, gm, small, wqkv, gs_att)

        def reduce(g):
            total = lax.psum_scatter(g, "dp", scatter_dimension=0, tiled=True)
            return lax.psum(total, "group").astype(F32)

        gqkv = gqkv.reshape(3, D, 3, THIRD).transpose(1, 2, 0, 3).reshape(D, 3 * D)
        gup = gup.transpose(1, 0, 2).reshape(D, FF)
        rqkv, rout, rup, rdown = [reduce(g) for g in (gqkv, gout, gup, gdown.reshape(FF, D))]
        gs = lax.psum(gs_mlp + gs_qkv, ("group", "dp"))

        def own(first, count):
            flat = gs[first : first + count].reshape(dp, -1)
            return lax.dynamic_index_in_dim(flat, p, 0, keepdims=False)

        tinies = [own(first, v.shape[0] * dp // D) for first, v in zip(SMALL_ROWS, vectors)]

    g1, s1, qb, fr, ob, g2, s2, ub, db = tinies
    act, gin = act.reshape(images.shape), gin.reshape(images.shape)
    return (act, gin, g1, s1, rqkv, qb, fr, rout, ob, g2, s2, rup, ub, rdown, db)


def solution(mesh):
    batch = P(("group", "dp"), None, None)
    per_image = P(("group", "dp"))
    vec, mat = P("dp"), P("dp", None)
    fast = dict(mesh.shape) == {"group": 4, "dp": 8}
    return jax.shard_map(
        functools.partial(on_device, fast),
        mesh=mesh,
        in_specs=(batch, batch, per_image, per_image, P(), vec, vec, mat, vec, vec, mat, vec, vec, vec, mat, vec, mat, vec),
        out_specs=(batch, batch, vec, vec, mat, vec, vec, mat, vec, vec, vec, mat, vec, mat, vec),
        check_vma=False,
    )
```

profile of v0, /device:TPU:0, one launch (start us, length us, event | category | flops | bytes accessed | tf_op | source)
XLA Modules:
  0.0 269.1 jit_solution(15920990923895026407)
XLA Ops:
  0.6 1.2 reshape.71.refs_2_
  1.9 1.2 reshape.76.refs_7_
  3.1 75.4 %forward.1 = (bf16[1152,2304]{1,0:T(8,128)(2,1)}, bf16[1152,768]{1,0:T(8,128)(2,1)}, f32[1152,768]{1,0:T(8,128)}, f32[1152,768]{1,0:T(8,128)}, bf16[1152,768]{1,...) custom-call(s32[2]{0:T(128)} %side_ref.5, ...), custom_call_target="tpu_custom_call" | custom-call | tf_op jit(solution)/shard_map/forward/pallas_call | solution.py:1253
  78.5 79.8 %mlp.1 = (f32[1152,768]{1,0:T(8,128)}, f32[1152,768]{1,0:T(8,128)}, bf16[1152,768]{1,0:T(8,128)(2,1)}, bf16[2,1024,768]{2,1,0:T(8,128)(2,1)}, bf16[2,768,1024]{2...) custom-call(s32[2]{0:T(128)} %side_ref.5, ...), custom_call_target="tpu_custom_call" | custom-call | tf_op jit(solution)/shard_map/mlp/pallas_call | solution.py:1308
  158.3 70.0 %attend_back.1 = (bf16[1152,2304]{1,0:T(8,128)(2,1)}, f32[16,768]{1,0:T(8,128)}, f32[128,768]{1,0:T(8,128)}, f32[96,1024]{1,0:T(8,128)}, f32[128,768]{1,0:T(8,12...) custom-call(s32[2]{0:T(128)} %side_ref.5, s32[2]{0:T(128)} %assign_ref.5, ...), custom_call_target="tpu_custom_call" | custom-call | tf_op jit(solution)/shard_map/attend_back/pallas_call | solution.py:1336
  228.3 31.7 %project_back.1 = (f32[1152,768]{1,0:T(8,128)}, f32[16,768]{1,0:T(8,128)}, f32[96,768]{1,0:T(8,128)}) custom-call(s32[2]{0:T(128)} %assign_ref.5, s32[4]{0:T(128)} %counts_ref.5, f32[16,768]{1,0:T(8,128)} %get-tuple-element.64.small.small_ref, f32[16,768]{1,0:T(8,128)} %get-tuple-element.80.gs_att, f32[16,768]{1,0:T(8,128)} %get-tuple-element.81.gs_mlp, ...), custom_call_target="tpu_custom_call" | custom-call | tf_op jit(solution)/shard_map/project_back/pallas_call | solution.py:1348
  260.0 8.9 %finish.1 = (f32[1152,768]{1,0:T(8,128)}, f32[1152,768]{1,0:T(8,128)}, f32[96,2304]{1,0:T(8,128)}, f32[96,768]{1,0:T(8,128)}, f32[96,3072]{1,0:T(8,128)}, /*inde...) custom-call(f32[16,768]{1,0:T(8,128)} %get-tuple-element.85.gs, ...), custom_call_target="tpu_custom_call" | custom-call | tf_op jit(solution)/shard_map/finish/pallas_call | solution.py:1368
where the time goes:
time: 269 us
  Pallas kernels  266 us (99%)
    pallas_call x1, Pallas kernels, on_device(): pl.pallas_call(functools.partial(mlp_moving, n, slots), out_shape=firsts...  79.8 us
    pallas_call x1, Pallas kernels, on_device(): pl.pallas_call(functools.partial(forward_gather, n), out_shape=kept + [sd...  75.4 us
    pallas_call x1, Pallas kernels, on_device(): pl.pallas_call(functools.partial(attend_back_reduce, n, slots), out_shape...  70 us
    pallas_call x1, Pallas kernels, on_device(): pl.pallas_call(functools.partial(qkv_back_reduce, n, slots), out_shape=[s...  31.7 us
    pallas_call x1, Pallas kernels, on_device(): pl.pallas_call(functools.partial(finish_kernel, dp, 'dp'), out_shape=[sds...  8.92 us

commit v1 on v0

--- a/solution.py
+++ b/solution.py
@@ -785,6 +785,16 @@
     n2t[...] = n2[...].T
     hooks("entered")
 
+    first = pl.ds(0, 256)
+    hid[:, first] = jnp.zeros((rows_all, 256), BF)
+    gpre[:, first] = jnp.zeros((rows_all, 256), BF)
+
+    def weights(step):
+        c = step // BLOCKS
+        cols = pl.ds(pl.multiple_of((step % BLOCKS) * 256, 256), 256)
+        gdown[c, cols, :] = (dot(hid[:, cols], bl[...], TN) * scale).astype(BF)
+        gup[c, :, cols] = (dot(n2t[...], gpre[:, cols], NN) * scale).astype(BF)
+
     def block(step, _):
         hooks("block", step)
         c, k = step // BLOCKS, step % BLOCKS
@@ -792,11 +802,12 @@
         bias = ubias[pl.ds(step, 1), :]
         wuc = wu[c, :, cols]
         wdc = wd[c, cols, :]
+        weights(jnp.maximum(step - 1, 0))
+        pieces = [pl.ds(i * tile, tile) for i in range(2 * images)]
+        pres = [dot(n2[rows], wuc, NN) + bias for rows in pieces]
+        backs = [dot(bl[rows], wdc, NT) for rows in pieces]
         bsum = None
-        for i in range(images):
-            rows = pl.ds(i * SLOT, SLOT)
-            pre = dot(n2[rows], wuc, NN) + bias
-            back = dot(bl[rows], wdc, NT)
+        for rows, pre, back in zip(pieces, pres, backs):
             value, slope = gelu_pair(pre)
             hid[rows, cols] = value.astype(BF)
             g = (back * slope).astype(BF)
@@ -804,22 +815,21 @@
             part = jnp.sum(g.astype(F32), axis=0, keepdims=True)
             bsum = part if bsum is None else bsum + part
         gubias[pl.ds(step, 1), :] = bsum
-        gdown[c, cols, :] = (dot(hid[:, cols], bl[...], TN) * scale).astype(BF)
-        gup[c, :, cols] = (dot(n2t[...], gpre[:, cols], NN) * scale).astype(BF)
 
         @pl.when(k == BLOCKS - 1)
         def _():
             def tail(n, _):
-                rows = pl.ds(pl.multiple_of(n * tile, tile), tile)
+                rows = pl.ds(pl.multiple_of(n * SLOT, SLOT), SLOT)
                 act[rows] += dot(hid[rows], wd[c], NN)
                 gm[rows] += dot(gpre[rows], wu[c], NT)
                 return 0
 
-            lax.fori_loop(0, 2 * images, tail, 0)
+            lax.fori_loop(0, images, tail, 0)
 
         return 0
 
     lax.fori_loop(0, PARTS * BLOCKS, block, 0)
+    weights(PARTS * BLOCKS - 1)
     hooks("blocks")
 
     def leave(step, _):
@@ -939,10 +949,10 @@
 
 
 MLP_PLAN = {
-    "u": (1, 4, 7, 9, 9),
-    "d": (0, 1, 4, 6, 8),
-    "rd": (5, 6, 8, 9, 11, 13, 14),
-    "ru": (6, 8, 10, 12, 13, 14, 14),
+    "u": (0, 2, 4, 5, 7),
+    "d": (1, 4, 5, 7, 8),
+    "rd": (6, 8, 10, 12, 13, 14, 14),
+    "ru": (6, 7, 9, 11, 13, 14, 14),
 }
 
 
@@ -1044,48 +1054,6 @@
     attend_back_compute(images, 3, side_ref, device_weight(slots, assign_ref, counts_ref), ins, norm, gproj, gws, gs, gf, lambda *a: None)
 
 
-def attend_back_reduce(images, slots, side_ref, assign_ref, counts_ref, *refs):
-    ins_in, norm_in, (gd, gu, go) = refs[0:5], refs[5], refs[6:9]
-    gproj_out, gs, outs = refs[9], refs[10], refs[11:18]
-    ins, norm, gproj, gws, gf = refs[18:23], refs[23], refs[24], refs[25], refs[26]
-    bufs, (load_sems, local, send, recv) = refs[27:69], refs[69:73]
-    w = Place()
-    srcs = (gd.at[0], gu.at[0], gd.at[1], gu.at[1], go, gws.at[0], gws.at[1])
-    items = {
-        name: Reduce(w, srcs[i], bufs[6 * i : 6 * i + 6], outs[i], local.at[i], send.at[i], recv.at[i])
-        for i, name in enumerate(BACK_PLAN)
-    }
-    moves = Moves(items, BACK_PLAN)
-
-    def hooks(where, step=None):
-        if where == "start":
-            copies = [load(src, dst, load_sems.at[i]) for i, (src, dst) in enumerate(zip(ins_in + (norm_in,), ins + (norm,)))]
-            greet(w.partners())
-            moves.at(0)
-            for copy in copies:
-                copy.wait()
-        elif where == "step":
-            moves.within(step + 1, 1, 12)
-        else:
-            copy = load(gproj, gproj_out, load_sems.at[0])
-            moves.at(13)
-            moves.at(14)
-            copy.wait()
-
-    attend_back_compute(images, 2, side_ref, device_weight(slots, assign_ref, counts_ref), ins, norm, gproj, gws, gs, gf, hooks)
-
-
-BACK_PLAN = {
-    "d1": (3, 4, 7, 9, 11, 14, 14),
-    "u1": (0, 2, 4, 8, 10, 13, 13),
-    "d2": (1, 3, 5, 8, 10, 12, 12),
-    "u2": (3, 7, 9, 10, 13, 14, 14),
-    "o": (0, 3, 7, 9, 11, 12, 13),
-    "q0": (5, 8, 10, 12, 13, 14, 14),
-    "q1": (9, 9, 11, 12, 13, 14, 14),
-}
-
-
 def qkv_back_compute(images, x_ref, gproj_ref, gm_ref, small_ref, w_ref, gs_in, gin_ref, gs_ref, hooks):
     hooks("start")
     gain = small_ref[R_G1 : R_G1 + 1]
@@ -1098,7 +1066,7 @@
         unit, inv = norm_stats(x_ref[rows])
         gn = None
         for c in range(3):
-            term = dot(gproj_ref[rows, c * D : (c + 1) * D], w_ref[c], NT)
+            term = dot(gproj_ref[rows, c * D : (c + 1) * D], w_ref[c][...], NT)
             gn = term if gn is None else gn + term
         gs_ref[R_G1 : R_G1 + 1] += jnp.sum(gn * unit, axis=0, keepdims=True)
         gs_ref[R_S1 : R_S1 + 1] += jnp.sum(gn, axis=0, keepdims=True)
@@ -1117,47 +1085,67 @@
         if where == "end":
             gs[...] = gs[...] * device_weight(slots, assign_ref, counts_ref)
 
-    qkv_back_compute(images, x_ref, gproj_ref, gm_ref, small_ref, w_ref, gs_in, gin, gs, hooks)
-
-
-def qkv_back_reduce(images, slots, assign_ref, counts_ref, small_ref, gs_att, gs_mlp, *refs):
-    ins_in, (gin, gs, out) = refs[0:5], refs[5:8]
-    norm, gproj, x, w_ref, gm = refs[8:13]
-    gw, bufs, tinybufs, (load_sems, local, send, recv, ssend, srecv) = refs[13], refs[14:20], refs[20], refs[21:27]
+    parts = [w_ref.at[c] for c in range(3)]
+    qkv_back_compute(images, x_ref, gproj_ref, gm_ref, small_ref, parts, gs_in, gin, gs, hooks)
+
+
+def backward_reduce(images, slots, side_ref, assign_ref, counts_ref, small_ref, gs_mlp, *refs):
+    ins_in, (gd, gu, go), (x_in, gm_in, w_in) = refs[0:6], refs[6:9], refs[9:12]
+    gin_out, gs, outs = refs[12], refs[13], refs[14:22]
+    ins, gproj, gws, gf, gs_own = refs[22:28], refs[28], refs[29], refs[30], refs[31]
+    bufs, tinybufs, (loads, local, send, recv, ssend, srecv) = refs[32:80], refs[80], refs[81:87]
+    qkv, cos, sin, norm = ins[0], ins[3], ins[4], ins[5]
     w = Place()
-    last = Reduce(w, gw, bufs, out, local, send, recv)
+    weight = device_weight(slots, assign_ref, counts_ref)
+    srcs = (gd.at[0], gu.at[0], gd.at[1], gu.at[1], go, gws.at[0], gws.at[1], gws.at[2])
+    items = {
+        name: Reduce(w, srcs[i], bufs[6 * i : 6 * i + 6], outs[i], local.at[i], send.at[i], recv.at[i])
+        for i, name in enumerate(BACK_PLAN)
+    }
+    moves = Moves(items, BACK_PLAN)
     tiny = SmallSum(w, gs, tinybufs, ssend, srecv)
-    weight = device_weight(slots, assign_ref, counts_ref)
-
-    def hooks(where, index=None):
+
+    def hooks(where, step=None):
         if where == "start":
-            copies = [load(src, dst, load_sems.at[i]) for i, (src, dst) in enumerate(zip(ins_in, refs[8:13]))]
+            copies = [load(src, dst, loads.at[i]) for i, (src, dst) in enumerate(zip(ins_in, ins))]
             greet(w.partners() + [(w.g ^ 3, w.p)])
-            copies[0].wait()
-            copies[1].wait()
-            weight_third(2, weight, norm, gproj, gw)
-            last.stage(0)
-            for copy in copies[2:]:
+            moves.at(0)
+            for copy in copies:
                 copy.wait()
-        elif where == "tile":
-            for number, when in ((1, 1), (2, 3)):
-
-                @pl.when(index == when)
-                def _(number=number):
-                    last.stage(number)
-
-        else:
-            gs[...] = gs[...] * weight + gs_mlp[...]
-            tiny.stage(0)
-            last.stage(3)
-            tiny.stage(1)
-            last.stage(4)
-            tiny.stage(2)
-            last.stage(5)
-            tiny.stage(3)
-            last.stage(6)
-
-    qkv_back_compute(images, x, gproj, gm, small_ref, w_ref, gs_att, gin, gs, hooks)
+        elif where == "step":
+            moves.within(step + 1, 1, 12)
+
+    attend_back_compute(images, 3, side_ref, weight, ins[0:5], norm, gproj, gws, gs_own, gf, hooks)
+    copies = [load(x_in, cos, loads.at[0]), load(gm_in, sin, loads.at[1])]
+    wide = [qkv.at[pl.ds(0, D), pl.ds(c * D, D)] for c in range(3)]
+    copies += [load(w_in.at[c], wide[c], loads.at[2 + c]) for c in range(3)]
+    moves.at(13)
+    for copy in copies:
+        copy.wait()
+
+    def tiles(where, step=None):
+        if where == "tile":
+            moves.within(step + 14, 14, 17)
+
+    qkv_back_compute(images, cos, gproj, sin, small_ref, wide, gs_own, sin, gs, tiles)
+    copy = load(sin, gin_out, loads.at[0])
+    gs[...] = gs[...] * weight + gs_mlp[...]
+    for number in range(4):
+        tiny.stage(number)
+        moves.at(18 + number)
+    copy.wait()
+
+
+BACK_PLAN = {
+    "d1": (1, 3, 6, 9, 17, 19, 19),
+    "u1": (1, 7, 11, 14, 18, 19, 21),
+    "d2": (2, 4, 6, 9, 13, 15, 19),
+    "u2": (2, 5, 8, 11, 14, 18, 20),
+    "o": (0, 4, 7, 13, 16, 18, 21),
+    "q0": (6, 7, 11, 15, 18, 19, 20),
+    "q1": (9, 10, 14, 16, 18, 19, 20),
+    "q2": (13, 14, 17, 18, 19, 20, 21),
+}
 
 
 def finish_kernel(dp, p_axis, gs, act_in, gin_in, rout_in, *refs):
@@ -1332,37 +1320,20 @@
             name="mlp",
         )(resolution, assignment, counts, small, x, cot, ctx, wo, wu, wd, up_later, down_later)
         third = (D // dp, D)
-        sizes = sizes + sizes + [third] * 3
-        gproj, gs_att, rdown1, rup1, rdown2, rup2, rout, rq0, rq1 = pl.pallas_call(
-            functools.partial(attend_back_reduce, n, slots),
-            out_shape=[gproj_shape] + rest + [sds(z, F32) for z in sizes],
-            in_specs=[smem] * 3 + [anyw] * 9,
-            out_specs=[anyw] + vm(8),
+        sizes = sizes + sizes + [third] * 4
+        gin, gs, rdown1, rup1, rdown2, rup2, rout, rq0, rq1, rq2 = pl.pallas_call(
+            functools.partial(backward_reduce, n, slots),
+            out_shape=[sds((rows, D), F32)] + rest + [sds(z, F32) for z in sizes],
+            in_specs=[smem] * 3 + vm(2) + [anyw] * 12,
+            out_specs=[anyw] + vm(9),
             scratch_shapes=tables
-            + [vmem((rows, D), BF), vmem((rows, 3 * D), BF), vmem((2, D, D), BF), vmem((8, D), F32)]
+            + [vmem((rows, D), BF), vmem((rows, 3 * D), BF), vmem((3, D, D), BF), vmem((8, D), F32)]
+            + [vmem((R_ALL, D), F32)]
             + sum([Reduce.buffers(*z) for z in sizes], [])
-            + [dma((6,)), dma((7,)), dma((7,)), dma((7, 6))],
+            + [vmem((12, R_ALL, D), F32), dma((6,)), dma((8,)), dma((8,)), dma((8, 6)), dma((3, 4)), dma((3, 4))],
             compiler_params=moving(1, 62),
-            name="attend_back",
-        )(resolution, assignment, counts, qkv, gctx, lse, cos, sin, norm1, gdown, gup, gout)
-        gin, gs, rq2 = pl.pallas_call(
-            functools.partial(qkv_back_reduce, n, slots),
-            out_shape=[sds((rows, D), F32)] + rest + [sds(third, F32)],
-            in_specs=[smem] * 2 + vm(3) + [anyw] * 5,
-            out_specs=vm(3),
-            scratch_shapes=[
-                vmem((rows, D), BF),
-                vmem((rows, 3 * D), BF),
-                vmem((rows, D), F32),
-                vmem((3, D, D), BF),
-                vmem((rows, D), F32),
-                vmem((D, D), BF),
-            ]
-            + Reduce.buffers(*third)
-            + [vmem((12, R_ALL, D), F32), dma((5,)), dma, dma, dma((6,)), dma((3, 4)), dma((3, 4))],
-            compiler_params=moving(2, 60),
-            name="project_back",
-        )(assignment, counts, small, gs_att, gs_mlp, norm1, gproj, x, wqkv, gm)
+            name="backward",
+        )(resolution, assignment, counts, small, gs_mlp, qkv, gctx, lse, cos, sin, norm1, gdown, gup, gout, x, gm, wqkv)
 
         matrices = (qkv_weight, out_weight, up_weight, down_weight)
         act, gin, rqkv, rout, rup, rdown, *tinies = pl.pallas_call(

time: 269 us -> 243 us (0.903)
  Pallas kernels: 266 us -> 240 us
    pallas_call x2 -> x1, Pallas kernels: 102 us -> 83.9 us  [on_device(): pl.pallas_call(functools.partial(backward_reduce, n, slots), out_shape=[s...]
    pallas_call x1, Pallas kernels: 79.8 us -> 71.6 us  [on_device(): pl.pallas_call(functools.partial(mlp_moving, n, slots), out_shape=firsts...]
where the time goes in v1:
time: 243 us
  Pallas kernels  240 us (99%)
  local copies, waits for them, and re-layouts  2.49 us (1%)
    pallas_call x1, Pallas kernels, on_device(): pl.pallas_call(functools.partial(backward_reduce, n, slots), out_shape=[s...  83.9 us
    pallas_call x1, Pallas kernels, on_device(): pl.pallas_call(functools.partial(forward_gather, n), out_shape=kept + [sd...  75.3 us
    pallas_call x1, Pallas kernels, on_device(): pl.pallas_call(functools.partial(mlp_moving, n, slots), out_shape=firsts...  71.6 us
    pallas_call x1, Pallas kernels, on_device(): pl.pallas_call(functools.partial(finish_kernel, dp, 'dp'), out_shape=[sds...  8.92 us

profile of v1, /device:TPU:0, one launch (start us, length us, event | category | flops | bytes accessed | tf_op | source)
XLA Modules:
  0.0 243.1 jit_solution(4726599457371177180)
XLA Ops:
  0.6 1.2 reshape.71.refs_2_
  1.9 1.2 reshape.76.refs_7_
  3.1 75.3 %forward.1 = (bf16[1152,2304]{1,0:T(8,128)(2,1)}, bf16[1152,768]{1,0:T(8,128)(2,1)}, f32[1152,768]{1,0:T(8,128)}, f32[1152,768]{1,0:T(8,128)}, bf16[1152,768]{1,...) custom-call(s32[2]{0:T(128)} %side_ref.5, ...), custom_call_target="tpu_custom_call" | custom-call | tf_op jit(solution)/shard_map/forward/pallas_call | solution.py:1241
  78.5 71.6 %mlp.1 = (f32[1152,768]{1,0:T(8,128)}, f32[1152,768]{1,0:T(8,128)}, bf16[1152,768]{1,0:T(8,128)(2,1)}, bf16[2,1024,768]{2,1,0:T(8,128)(2,1)}, bf16[2,768,1024]{2...) custom-call(s32[2]{0:T(128)} %side_ref.5, ...), custom_call_target="tpu_custom_call" | custom-call | tf_op jit(solution)/shard_map/mlp/pallas_call | solution.py:1296
  150.1 83.9 %backward.1 = (f32[1152,768]{1,0:T(8,128)}, f32[16,768]{1,0:T(8,128)}, f32[128,768]{1,0:T(8,128)}, f32[96,1024]{1,0:T(8,128)}, f32[128,768]{1,0:T(8,128)}, /*ind...) custom-call(s32[2]{0:T(128)} %side_ref.5, s32[2]{0:T(128)} %assign_ref.3, ...), custom_call_target="tpu_custom_call" | custom-call | tf_op jit(solution)/shard_map/backward/pallas_call | solution.py:1324
  234.0 8.9 %finish.1 = (f32[1152,768]{1,0:T(8,128)}, f32[1152,768]{1,0:T(8,128)}, f32[96,2304]{1,0:T(8,128)}, f32[96,768]{1,0:T(8,128)}, f32[96,3072]{1,0:T(8,128)}, /*inde...) custom-call(f32[16,768]{1,0:T(8,128)} %get-tuple-element.81.gs, ...), custom_call_target="tpu_custom_call" | custom-call | tf_op jit(solution)/shard_map/finish/pallas_call | solution.py:1339

commit v2 on v1

--- a/solution.py
+++ b/solution.py
@@ -285,6 +285,9 @@
     def add(self, target, *terms):
         def body(i, _):
             rows = pl.ds(pl.multiple_of(i * 32, 32), 32)
+            if len(terms) == 1:
+                target[rows] = target[rows] + terms[0][rows]
+                return 0
             total = target[rows].astype(F32)
             for term in terms:
                 total = total + term[rows].astype(F32)
@@ -607,13 +610,13 @@
 
 
 def compact(tinies, ref):
-    run = tinies[0].shape[1]
+    run = tinies[0].shape[0]
     first = {row: i for i, row in enumerate(SMALL_ROWS)}
     for n, row in enumerate(SINGLES):
-        ref[n : n + 1, :run] = tinies[first[row]][...].astype(BF).astype(F32)
+        ref[n, pl.ds(0, run)] = tinies[first[row]][...].astype(BF).astype(F32)
     for index, _, count, at in MORE:
         for m in range(count):
-            ref[at + m : at + m + 1, :run] = tinies[index][:, m * run : (m + 1) * run].astype(BF).astype(F32)
+            ref[at + m, pl.ds(0, run)] = tinies[index][pl.ds(m * run, run)].astype(BF).astype(F32)
 
 
 def expand(parts, small, run):
@@ -769,6 +772,7 @@
         return pl.ds(pl.multiple_of(step * tile, tile), tile), slot < side * side
 
     def enter(step, _):
+        hooks("enter", step)
         rows, valid = tile_rows(step)
         middle = mid[rows] + (dot(ctx_ref[rows], wo_ref[...], NN) + small[R_OB : R_OB + 1])
         mid[rows] = middle
@@ -848,6 +852,7 @@
         bl[rows] = low
         gs[R_OB : R_OB + 1] += jnp.sum(low.astype(F32), axis=0, keepdims=True)
         gctx[rows] = dot(low, wo_ref[...], NT).astype(BF)
+        hooks("left", step)
         return 0
 
     lax.fori_loop(0, 2 * images, leave, 0)
@@ -882,7 +887,7 @@
     refs = rest[17:25]
     mid, n2, n2t = refs[0], refs[1], refs[2]
     cot, ctx, wo, wu, wd, act, gm, gd, gu = rest[25:34]
-    bufs, (local, sems, recv, rlocal, rsend, rrecv) = rest[34:46], rest[46:52]
+    bufs, (local, sems, recv, rlocal, rsend, rrecv, tile_in, tile_out) = rest[34:46], rest[46:54]
     w = Place()
     last = PARTS - 1
     items = {
@@ -898,9 +903,24 @@
         keep.append(load(src, dst, local.at[len(keep)]))
         return keep[-1]
 
+    tile = SLOT // 2
+
+    def by_tile(step, pairs, sem):
+        rows = pl.ds(pl.multiple_of(step * tile, tile), tile)
+        return [pltpu.make_async_copy(src.at[rows], dst.at[rows], sem.at[i, step]) for i, (src, dst) in enumerate(pairs)]
+
+    def arriving(step):
+        return by_tile(step, ((ctx_in, ctx), (x_in, mid), (cot_in, cot)), tile_in)
+
+    def leaving(step):
+        return by_tile(step, ((act, act_out), (gm, gm_out), (n2, gctx_out)), tile_out)
+
     def hooks(where, step=None):
         if where == "start":
-            move(ctx_in, ctx), move(x_in, mid), move(wo_in, wo), move(cot_in, cot)
+            move(wo_in, wo)
+            for i in range(2 * images):
+                for copy in arriving(i):
+                    copy.start()
             for c in range(last):
                 move(wu_in.at[c], wu.at[c])
                 move(wd_in.at[c], wd.at[c])
@@ -909,10 +929,15 @@
                 move(own, full.at[last, pl.ds(pl.multiple_of(w.p * count, 16), count)])
             greet(w.partners())
             moves.at(0)
-            for copy in keep[:4]:
+            keep[0].wait()
+        elif where == "enter":
+            for copy in arriving(step):
                 copy.wait()
+        elif where == "left":
+            for copy in leaving(step):
+                copy.start()
         elif where == "entered":
-            for copy in keep[4:]:
+            for copy in keep[1:]:
                 copy.wait()
             keep.clear()
         elif where == "block":
@@ -923,11 +948,11 @@
                 move(gu.at[c], gu_out.at[c - 1])
             moves.at(13)
         else:
-            move(act, act_out)
-            move(gm, gm_out)
-            move(n2, gctx_out)
             move(n2t.at[:, pl.ds(0, D)], go_out)
             moves.at(14)
+            for i in range(2 * images):
+                for copy in leaving(i):
+                    copy.wait()
             for copy in keep:
                 copy.wait()
 
@@ -1105,20 +1130,39 @@
     moves = Moves(items, BACK_PLAN)
     tiny = SmallSum(w, gs, tinybufs, ssend, srecv)
 
+    def third(c):
+        copies = []
+        for i, width in ((0, D), (1, THIRD), (3, THIRD), (4, THIRD)):
+            lanes = pl.ds(c * width, width)
+            copies.append(pltpu.make_async_copy(ins_in[i].at[:, lanes], ins[i].at[:, lanes], loads.at[c, i]))
+        whole = {0: 2, 1: 5}.get(c)
+        if whole is not None:
+            copies.append(pltpu.make_async_copy(ins_in[whole], ins[whole], loads.at[c, 5]))
+        return copies
+
     def hooks(where, step=None):
         if where == "start":
-            copies = [load(src, dst, loads.at[i]) for i, (src, dst) in enumerate(zip(ins_in, ins))]
+            for c in range(3):
+                for copy in third(c):
+                    copy.start()
             greet(w.partners() + [(w.g ^ 3, w.p)])
             moves.at(0)
-            for copy in copies:
+            for copy in third(0):
                 copy.wait()
         elif where == "step":
+            for c, when in ((1, 2 * images - 1), (2, 4 * images)):
+
+                @pl.when(step == when)
+                def _(c=c):
+                    for copy in third(c):
+                        copy.wait()
+
             moves.within(step + 1, 1, 12)
 
     attend_back_compute(images, 3, side_ref, weight, ins[0:5], norm, gproj, gws, gs_own, gf, hooks)
-    copies = [load(x_in, cos, loads.at[0]), load(gm_in, sin, loads.at[1])]
+    copies = [load(x_in, cos, loads.at[0, 0]), load(gm_in, sin, loads.at[0, 1])]
     wide = [qkv.at[pl.ds(0, D), pl.ds(c * D, D)] for c in range(3)]
-    copies += [load(w_in.at[c], wide[c], loads.at[2 + c]) for c in range(3)]
+    copies += [load(w_in.at[c], wide[c], loads.at[0, 2 + c]) for c in range(3)]
     moves.at(13)
     for copy in copies:
         copy.wait()
@@ -1128,7 +1172,7 @@
             moves.within(step + 14, 14, 17)
 
     qkv_back_compute(images, cos, gproj, sin, small_ref, wide, gs_own, sin, gs, tiles)
-    copy = load(sin, gin_out, loads.at[0])
+    copy = load(sin, gin_out, loads.at[0, 0])
     gs[...] = gs[...] * weight + gs_mlp[...]
     for number in range(4):
         tiny.stage(number)
@@ -1267,7 +1311,7 @@
             ],
             compiler_params=moving(0, 56),
             name="forward",
-        )(resolution, *[v.reshape(1, -1) for v in vectors], x, *weights)
+        )(resolution, *vectors, x, *weights)
         qkv, norm1, cos, sin, ctx, lse, small, wqkv, wo, wu, wd, up_later, down_later = outs
     else:
         packed = [place_rows(p, dp, lax.reduce_precision(v, 8, 7)) for v in vectors]
@@ -1315,7 +1359,8 @@
                 vmem((PARTS, D, part), BF),
             ]
             + sum([Reduce.buffers(*z) for z in sizes], [])
-            + [dma((12,)), dma((4,)), dma((2, 16)), dma((2,)), dma((2,)), dma((2, 6))],
+            + [dma((12,)), dma((4,)), dma((2, 16)), dma((2,)), dma((2,)), dma((2, 6))]
+            + [dma((3, 2 * n))] * 2,
             compiler_params=moving(3, 63),
             name="mlp",
         )(resolution, assignment, counts, small, x, cot, ctx, wo, wu, wd, up_later, down_later)
@@ -1330,7 +1375,7 @@
             + [vmem((rows, D), BF), vmem((rows, 3 * D), BF), vmem((3, D, D), BF), vmem((8, D), F32)]
             + [vmem((R_ALL, D), F32)]
             + sum([Reduce.buffers(*z) for z in sizes], [])
-            + [vmem((12, R_ALL, D), F32), dma((6,)), dma((8,)), dma((8,)), dma((8, 6)), dma((3, 4)), dma((3, 4))],
+            + [vmem((12, R_ALL, D), F32), dma((3, 6)), dma((8,)), dma((8,)), dma((8, 6)), dma((3, 4)), dma((3, 4))],
             compiler_params=moving(1, 62),
             name="backward",
         )(resolution, assignment, counts, small, gs_mlp, qkv, gctx, lse, cos, sin, norm1, gdown, gup, gout, x, gm, wqkv)

time: 243 us -> 237 us (0.975)
  Pallas kernels: 240 us -> 236 us
  local copies, waits for them, and re-layouts: 2.49 us -> 0 us
    pallas_call x1, Pallas kernels: 83.9 us -> 80.8 us  [on_device(): pl.pallas_call(functools.partial(backward_reduce, n, slots), out_shape=[s...]
    reshape x2 -> x0, local copies, waits for them, and re-layouts: 2.49 us -> none  [on_device(): v.reshape(1, -1)]
where the time goes in v2:
time: 237 us; the launch traced here: 236 us
  Pallas kernels  236 us (100%)
    pallas_call x1, Pallas kernels, on_device(): pl.pallas_call(functools.partial(backward_reduce, n, slots), out_shape=[s...  80.8 us
    pallas_call x1, Pallas kernels, on_device(): pl.pallas_call(functools.partial(forward_gather, n), out_shape=kept + [sd...  75.4 us
    pallas_call x1, Pallas kernels, on_device(): pl.pallas_call(functools.partial(mlp_moving, n, slots), out_shape=firsts...  70.5 us
    pallas_call x1, Pallas kernels, on_device(): pl.pallas_call(functools.partial(finish_kernel, dp, 'dp'), out_shape=[sds...  8.92 us

profile of v2, /device:TPU:0, one launch (start us, length us, event | category | flops | bytes accessed | tf_op | source)
XLA Modules:
  0.0 236.5 jit_solution(556728273781128811)
XLA Ops:
  0.7 75.4 %forward.1 = (bf16[1152,2304]{1,0:T(8,128)(2,1)}, bf16[1152,768]{1,0:T(8,128)(2,1)}, f32[1152,768]{1,0:T(8,128)}, f32[1152,768]{1,0:T(8,128)}, bf16[1152,768]{1,...) custom-call(s32[2]{0:T(128)} %side_ref.5, ...), custom_call_target="tpu_custom_call" | custom-call | tf_op jit(solution)/shard_map/forward/pallas_call | solution.py:1285
  76.0 70.5 %mlp.1 = (f32[1152,768]{1,0:T(8,128)}, f32[1152,768]{1,0:T(8,128)}, bf16[1152,768]{1,0:T(8,128)(2,1)}, bf16[2,1024,768]{2,1,0:T(8,128)(2,1)}, bf16[2,768,1024]{2...) custom-call(s32[2]{0:T(128)} %side_ref.5, ...), custom_call_target="tpu_custom_call" | custom-call | tf_op jit(solution)/shard_map/mlp/pallas_call | solution.py:1340
  146.5 80.8 %backward.1 = (f32[1152,768]{1,0:T(8,128)}, f32[16,768]{1,0:T(8,128)}, f32[128,768]{1,0:T(8,128)}, f32[96,1024]{1,0:T(8,128)}, f32[128,768]{1,0:T(8,128)}, /*ind...) custom-call(s32[2]{0:T(128)} %side_ref.5, s32[2]{0:T(128)} %assign_ref.3, ...), custom_call_target="tpu_custom_call" | custom-call | tf_op jit(solution)/shard_map/backward/pallas_call | solution.py:1369
  227.4 8.9 %finish.1 = (f32[1152,768]{1,0:T(8,128)}, f32[1152,768]{1,0:T(8,128)}, f32[96,2304]{1,0:T(8,128)}, f32[96,768]{1,0:T(8,128)}, f32[96,3072]{1,0:T(8,128)}, /*inde...) custom-call(f32[16,768]{1,0:T(8,128)} %get-tuple-element.81.gs, ...), custom_call_target="tpu_custom_call" | custom-call | tf_op jit(solution)/shard_map/finish/pallas_call | solution.py:1384

commit v3 on v2

--- a/solution.py
+++ b/solution.py
@@ -531,8 +531,9 @@
     lax.fori_loop(0, images * SLOT // 192, body, 0)
 
 
-def angle_tables(images, side_ref, small, cos_ref, sin_ref):
+def angle_tables(images, side_ref, small, cos_ref, sin_ref, hooks):
     for j in range(D // 128):
+        hooks("table", j)
         flat = [small[R_FR : R_FR + 1, n + j // 2 * 128 : n + j // 2 * 128 + 128] for n in (0, D // 2)]
         fc, fr = [dot(jnp.broadcast_to(v, (8, 128)).astype(BF), spread(j % 2), NN)[0:1] for v in flat]
 
@@ -569,7 +570,7 @@
     hooks("start")
     norm_rows(images, x_ref, small, norm)
     hooks("tables")
-    angle_tables(images, side_ref, small, cos, sin)
+    angle_tables(images, side_ref, small, cos, sin, hooks)
     blocks, pairs = 3 * images, 2 * images
 
     def body(step, _):
@@ -644,7 +645,9 @@
     w = Place()
     pairs = [(bq.at[c], wq.at[c]) for c in range(3)] + [(bo, wo)]
     pairs += [(own.at[c], full.at[c]) for c in range(PARTS - 1) for own, full in ((bu, wu), (bd, wd))]
-    gathers = dict(zip(("q0", "q1", "q2", "o", "u0", "d0", "u1", "d1"), pairs))
+    lanes = [pl.ds(part * THIRD, THIRD) for part in range(3)]
+    gathers = [(bq.at[0, :, cols], wq.at[0, :, cols]) for cols in lanes] + pairs[1:]
+    gathers = dict(zip(("a0", "a1", "a2", "q1", "q2", "o", "u0", "d0", "u1", "d1"), gathers))
     gathers = {k: Gather(w, *v, sems, recv, i) for i, (k, v) in enumerate(gathers.items())}
     moves = Moves(gathers, FORWARD_PLAN)
     peers = [w.p ^ k for k in range(1, 8)]
@@ -702,8 +705,9 @@
             expand([(w.p, slots.at[0])] + [(peers[k - 1], slots.at[k]) for k in range(1, 8)], small, D // 8)
             moves.at(0)
         elif where == "tables":
-            moves.at(1)
             store("norm", norm, norm_out)
+        elif where == "table":
+            moves.at(1 + step / 10)
         elif where == "step":
 
             @pl.when(step == 0)
@@ -736,14 +740,16 @@
 
 
 FORWARD_PLAN = {
-    "q0": (-1, 1, 2, 2, 2),
-    "q1": (0, 2, 9, 11, 12),
-    "q2": (1, 4, 10, 16, 19),
-    "o": (1, 7, 14, 29, 31),
-    "u0": (3, 11, 17, 25, 26),
-    "d0": (5, 16, 21, 27, 31),
-    "u1": (17, 21, 28, 31, 32),
-    "d1": (10, 16, 24, 30, 31),
+    "a0": (-1, 1, 1.2, 1.4, 2),
+    "a1": (-1, 1, 1.2, 1.4, 4),
+    "a2": (-1, 1, 1.3, 1.5, 6),
+    "q1": (0, 1.5, 8, 11, 12),
+    "q2": (1, 6, 11, 17, 22),
+    "o": (1.5, 7, 13, 26, 32),
+    "u0": (3, 11, 19, 26, 32),
+    "d0": (7, 16, 20, 28, 32),
+    "u1": (13, 21, 26, 30, 32),
+    "d1": (8, 18, 24, 29, 32),
 }
 
 
@@ -1302,8 +1308,8 @@
             ]
             + [vmem(v.shape, F32) for v in weights]
             + [
-                dma((16,)),
-                dma((8, 16)),
+                dma((20,)),
+                dma((10, 16)),
                 dma((7,)),
                 dma((7,)),
                 dma((22,)),

time: 237 us -> 236 us (level)
  no operation moved by 1% of the time
where the time goes in v3:
time: 236 us; the launch traced here: 235 us
  Pallas kernels  234 us (99%)
    pallas_call x1, Pallas kernels, on_device(): pl.pallas_call(functools.partial(backward_reduce, n, slots), out_shape=[s...  79.5 us
    pallas_call x1, Pallas kernels, on_device(): pl.pallas_call(functools.partial(forward_gather, n), out_shape=kept + [sd...  75.8 us
    pallas_call x1, Pallas kernels, on_device(): pl.pallas_call(functools.partial(mlp_moving, n, slots), out_shape=firsts...  70.2 us
    pallas_call x1, Pallas kernels, on_device(): pl.pallas_call(functools.partial(finish_kernel, dp, 'dp'), out_shape=[sds...  8.92 us

profile of v3, /device:TPU:0, one launch (start us, length us, event | category | flops | bytes accessed | tf_op | source)
XLA Modules:
  0.0 235.2 jit_solution(14532402846129836777)
XLA Ops:
  0.7 75.8 %forward.1 = (bf16[1152,2304]{1,0:T(8,128)(2,1)}, bf16[1152,768]{1,0:T(8,128)(2,1)}, f32[1152,768]{1,0:T(8,128)}, f32[1152,768]{1,0:T(8,128)}, bf16[1152,768]{1,...) custom-call(s32[2]{0:T(128)} %side_ref.5, ...), custom_call_target="tpu_custom_call" | custom-call | tf_op jit(solution)/shard_map/forward/pallas_call | solution.py:1291
  76.4 70.2 %mlp.1 = (f32[1152,768]{1,0:T(8,128)}, f32[1152,768]{1,0:T(8,128)}, bf16[1152,768]{1,0:T(8,128)(2,1)}, bf16[2,1024,768]{2,1,0:T(8,128)(2,1)}, bf16[2,768,1024]{2...) custom-call(s32[2]{0:T(128)} %side_ref.5, ...), custom_call_target="tpu_custom_call" | custom-call | tf_op jit(solution)/shard_map/mlp/pallas_call | solution.py:1346
  146.6 79.5 %backward.1 = (f32[1152,768]{1,0:T(8,128)}, f32[16,768]{1,0:T(8,128)}, f32[128,768]{1,0:T(8,128)}, f32[96,1024]{1,0:T(8,128)}, f32[128,768]{1,0:T(8,128)}, /*ind...) custom-call(s32[2]{0:T(128)} %side_ref.5, s32[2]{0:T(128)} %assign_ref.3, ...), custom_call_target="tpu_custom_call" | custom-call | tf_op jit(solution)/shard_map/backward/pallas_call | solution.py:1375
  226.1 8.9 %finish.1 = (f32[1152,768]{1,0:T(8,128)}, f32[1152,768]{1,0:T(8,128)}, f32[96,2304]{1,0:T(8,128)}, f32[96,768]{1,0:T(8,128)}, f32[96,3072]{1,0:T(8,128)}, /*inde...) custom-call(f32[16,768]{1,0:T(8,128)} %get-tuple-element.81.gs, ...), custom_call_target="tpu_custom_call" | custom-call | tf_op jit(solution)/shard_map/finish/pallas_call | solution.py:1390

commit v4 on v3

--- a/solution.py
+++ b/solution.py
@@ -744,12 +744,12 @@
     "a1": (-1, 1, 1.2, 1.4, 4),
     "a2": (-1, 1, 1.3, 1.5, 6),
     "q1": (0, 1.5, 8, 11, 12),
-    "q2": (1, 6, 11, 17, 22),
+    "q2": (1, 7, 12, 18, 22),
     "o": (1.5, 7, 13, 26, 32),
-    "u0": (3, 11, 19, 26, 32),
-    "d0": (7, 16, 20, 28, 32),
-    "u1": (13, 21, 26, 30, 32),
-    "d1": (8, 18, 24, 29, 32),
+    "u0": (3, 12, 20, 27, 32),
+    "d0": (7, 17, 22, 29, 32),
+    "u1": (13, 23, 28, 31, 32),
+    "d1": (9, 20, 26, 30, 32),
 }
 
 

time: 236 us -> 236 us (level)
  no operation moved by 1% of the time
where the time goes in v4:
time: 236 us
  Pallas kernels  235 us (100%)
    pallas_call x1, Pallas kernels, on_device(): pl.pallas_call(functools.partial(backward_reduce, n, slots), out_shape=[s...  80.6 us
    pallas_call x1, Pallas kernels, on_device(): pl.pallas_call(functools.partial(forward_gather, n), out_shape=kept + [sd...  74.6 us
    pallas_call x1, Pallas kernels, on_device(): pl.pallas_call(functools.partial(mlp_moving, n, slots), out_shape=firsts...  71 us
    pallas_call x1, Pallas kernels, on_device(): pl.pallas_call(functools.partial(finish_kernel, dp, 'dp'), out_shape=[sds...  8.92 us

profile of v4, /device:TPU:0, one launch (start us, length us, event | category | flops | bytes accessed | tf_op | source)
XLA Modules:
  0.0 236.0 jit_solution(9226706731498464294)
XLA Ops:
  0.7 74.6 %forward.1 = (bf16[1152,2304]{1,0:T(8,128)(2,1)}, bf16[1152,768]{1,0:T(8,128)(2,1)}, f32[1152,768]{1,0:T(8,128)}, f32[1152,768]{1,0:T(8,128)}, bf16[1152,768]{1,...) custom-call(s32[2]{0:T(128)} %side_ref.5, ...), custom_call_target="tpu_custom_call" | custom-call | tf_op jit(solution)/shard_map/forward/pallas_call | solution.py:1291
  75.3 71.0 %mlp.1 = (f32[1152,768]{1,0:T(8,128)}, f32[1152,768]{1,0:T(8,128)}, bf16[1152,768]{1,0:T(8,128)(2,1)}, bf16[2,1024,768]{2,1,0:T(8,128)(2,1)}, bf16[2,768,1024]{2...) custom-call(s32[2]{0:T(128)} %side_ref.5, ...), custom_call_target="tpu_custom_call" | custom-call | tf_op jit(solution)/shard_map/mlp/pallas_call | solution.py:1346
  146.3 80.6 %backward.1 = (f32[1152,768]{1,0:T(8,128)}, f32[16,768]{1,0:T(8,128)}, f32[128,768]{1,0:T(8,128)}, f32[96,1024]{1,0:T(8,128)}, f32[128,768]{1,0:T(8,128)}, /*ind...) custom-call(s32[2]{0:T(128)} %side_ref.5, s32[2]{0:T(128)} %assign_ref.3, ...), custom_call_target="tpu_custom_call" | custom-call | tf_op jit(solution)/shard_map/backward/pallas_call | solution.py:1375
  226.9 8.9 %finish.1 = (f32[1152,768]{1,0:T(8,128)}, f32[1152,768]{1,0:T(8,128)}, f32[96,2304]{1,0:T(8,128)}, f32[96,768]{1,0:T(8,128)}, f32[96,3072]{1,0:T(8,128)}, /*inde...) custom-call(f32[16,768]{1,0:T(8,128)} %get-tuple-element.81.gs, ...), custom_call_target="tpu_custom_call" | custom-call | tf_op jit(solution)/shard_map/finish/pallas_call | solution.py:1390
